TPU v7x, 128 devices: a whole 4x4x4 slice. The times are simulated.
128 devices in a mesh: obs: 8 (over z_hi, y), unk: 16 (over z_lo, x, core).
Axes of the slice: x: 4, y: 4, z: 4 (z_hi: 2, z_lo: 2; z = z_hi * 2 + z_lo), core: 2. Of those that a mesh axis runs over, the one named last changes fastest.
Arguments:
- design: float32 [8192, 24576], P('obs', 'unk'), may hold values from -0.0625 to 0.0625
- weights: float32 [8192], P('obs'), may hold values from 0.25 to 4
Outputs:
- factor: float32 [24576, 1024], P(('unk', 'obs'))
All inputs are finite; a program needn't handle non-finite values.
Results may differ from a plain program's by a relative error of at most 0.00011.
Values sent between devices are 32-bit elements; how exact they have to be, the bound alone decides.
No kernel may reach another device: no remote copies, remote signals or barrier semaphores. Data moves between devices by JAX's collectives and lax.ppermute only.
A program may use at most 128 MiB of HBM per device.

v0:
```python
import jax, jax.numpy as jnp
from jax import lax
from jax.experimental import pallas as pl
from jax.experimental.pallas import tpu as pltpu
from jax.sharding import PartitionSpec as P

BLOCK = 128
SUB = 8
STRIP = 32


def split(x):
    hi = x.astype(jnp.bfloat16)
    return hi, (x - hi.astype(jnp.float32)).astype(jnp.bfloat16)


def dot_t(a, b):
    return lax.dot_general(a, b, (((1,), (1,)), ((), ())), preferred_element_type=jnp.float32)


def dot3_t(a, b):
    (ah, al), (bh, bl) = a, b
    return dot_t(ah, bh) + (dot_t(ah, bl) + dot_t(al, bh))


def on_lanes(value, lane):
    return jnp.broadcast_to(value[:, lane : lane + 1], (SUB, BLOCK))


def invert_diag(block_ref, inv_ref, stage, rows_ref):
    lane = lax.broadcasted_iota(jnp.int32, (SUB, BLOCK), 1)
    panels = BLOCK // SUB
    groups = [block_ref[q * SUB : (q + 1) * SUB, :] for q in range(panels)]
    natural, carried = None, None
    for p in range(panels):
        r0 = p * SUB
        base = (p % 2) * 3 * SUB * SUB
        one = lambda row: stage[pl.ds(base + row, SUB, stride=0), :]
        panel = groups[p]
        columns = [on_lanes(panel, r0 + c) for c in range(SUB)]
        if natural is not None:
            for i in range(SUB):
                stage[base + i * SUB : base + (i + 1) * SUB, :] = on_lanes(natural, r0 + i)
            panel = jnp.where((lane >= r0 - SUB) & (lane < r0), 0.0, panel)
            for k in range(SUB):
                down = stage[pl.ds(base + k, SUB, stride=SUB), :]
                panel = panel - down * carried[k]
                for c in range(SUB):
                    columns[c] = columns[c] - down * one(c * SUB + k)
        inside = (lane >= r0) & (lane < r0 + SUB)
        sub = lax.broadcasted_iota(jnp.int32, (SUB, BLOCK), 0)
        panel = jnp.where(inside, jnp.where(lane == r0 + sub, 1.0, 0.0), panel)
        at = SUB * SUB
        for c in range(SUB):
            stage[base + at + c * SUB : base + at + (c + 1) * SUB, :] = columns[c]
        stage[base + 2 * at : base + 2 * at + SUB, :] = panel
        e = {(i, c): one(at + c * SUB + i) for c in range(SUB) for i in range(c + 1)}
        w = [one(2 * at + i) for i in range(SUB)]
        for c in range(SUB):
            inv = lax.rsqrt(e[c, c])
            w[c] = w[c] * inv
            u = {i: e[c, i] * inv for i in range(c + 1, SUB)}
            for i in range(c + 1, SUB):
                w[i] = w[i] - u[i] * w[c]
                for j in range(i, SUB):
                    e[i, j] = e[i, j] - u[i] * u[j]
            rows_ref[r0 + c : r0 + c + 1, :] = w[c][0:1, :]
        natural, carried = rows_ref[r0 : r0 + SUB, :], w
        inv_ref[r0 : r0 + SUB, :] = jnp.where(lane < r0 + SUB, natural, 0.0)
        if p + 2 < panels:
            for q in range(p + 2, panels):
                spare = 6 * SUB * SUB + (q % 2) * SUB * SUB
                for i in range(SUB):
                    stage[spare + i * SUB : spare + (i + 1) * SUB, :] = on_lanes(natural, q * SUB + i)
                groups[q] = jnp.where(inside, 0.0, groups[q])
                for k in range(SUB):
                    groups[q] = groups[q] - stage[pl.ds(spare + k, SUB, stride=SUB), :] * w[k]


def unpack(where_ref, mine_ref, other_ref, work, pieces):
    count = mine_ref.shape[0]
    chip, core = where_ref[0], where_ref[1]
    for k in range(count):
        pieces[2 * (chip ^ k) + core] = mine_ref[k]
        pieces[2 * (chip ^ k) + 1 - core] = other_ref[k]
    for t in range(2 * count):
        low, high = t * STRIP, (4 * count - 1 - t) * STRIP
        cut, rest = (low // BLOCK + 1) * BLOCK, (high // BLOCK + 1) * BLOCK
        work[low : low + STRIP, :cut] = pieces[t, :, :cut]
        work[high : high + STRIP, :rest] = pieces[t, :, cut:]


def chol_kernel(where_ref, mine_ref, other_ref, low_ref, inv_ref, work, pieces, diag, dinv, hi_ref, lo_ref, stage, rows_ref):
    width = work.shape[0]
    blocks = width // BLOCK
    work[...] = jnp.zeros_like(work)
    unpack(where_ref, mine_ref, other_ref, work, pieces)

    def step(k, _):
        at = pl.multiple_of(k * BLOCK, BLOCK)
        diag[...] = work[pl.ds(at, BLOCK), pl.ds(at, BLOCK)]
        invert_diag(diag, dinv, stage, rows_ref)
        inverse = dinv[...]
        inv_ref[pl.ds(at, BLOCK), :] = inverse
        inverse = split(inverse)
        hi_ref[...] = jnp.zeros_like(hi_ref)
        lo_ref[...] = jnp.zeros_like(lo_ref)

        def below(i, _):
            rows = pl.ds(pl.multiple_of(i * BLOCK, BLOCK), BLOCK)
            new = dot3_t(split(work[rows, pl.ds(at, BLOCK)]), inverse)
            low_ref[rows, pl.ds(at, BLOCK)] = new
            hi, lo = split(new)
            hi_ref[rows, :] = hi
            lo_ref[rows, :] = lo
            return 0

        lax.fori_loop(k + 1, blocks, below, 0)

        def trail(i, _):
            rows = pl.ds(pl.multiple_of(i * BLOCK, BLOCK), BLOCK)
            work[rows, :] = work[rows, :] - dot3_t(
                (hi_ref[rows, :], lo_ref[rows, :]), (hi_ref[...], lo_ref[...])
            )
            return 0

        lax.fori_loop(k + 1, blocks, trail, 0)
        return 0

    lax.fori_loop(0, blocks, step, 0)


def cholesky_parts(where, mine, other):
    count, strip, packed = mine.shape
    width = count * BLOCK
    vmem = pl.BlockSpec(memory_space=pltpu.VMEM)
    return pl.pallas_call(
        chol_kernel,
        out_shape=(
            jax.ShapeDtypeStruct((width, width), jnp.float32),
            jax.ShapeDtypeStruct((width, BLOCK), jnp.float32),
        ),
        in_specs=[pl.BlockSpec(memory_space=pltpu.SMEM), vmem, vmem],
        out_specs=(vmem, vmem),
        scratch_shapes=[
            pltpu.VMEM((width, width), jnp.float32),
            pltpu.VMEM((2 * count, strip, packed), jnp.float32),
            pltpu.VMEM((BLOCK, BLOCK), jnp.float32),
            pltpu.VMEM((BLOCK, BLOCK), jnp.float32),
            pltpu.VMEM((width, BLOCK), jnp.bfloat16),
            pltpu.VMEM((width, BLOCK), jnp.bfloat16),
            pltpu.VMEM((8 * SUB * SUB, BLOCK), jnp.float32),
            pltpu.VMEM((BLOCK, BLOCK), jnp.float32),
        ],
        compiler_params=pltpu.CompilerParams(vmem_limit_bytes=32 << 20),
        cost_estimate=pl.CostEstimate(flops=80_000_000_000, bytes_accessed=8 << 20, transcendentals=0),
    )(where, mine, other)


def solve_kernel(gram_ref, low_ref, inv_ref, out_ref):
    _, width = gram_ref.shape
    blocks = width // BLOCK
    out_ref[...] = gram_ref[...]
    for k in range(blocks):
        cols = slice(k * BLOCK, (k + 1) * BLOCK)
        new = dot3_t(split(out_ref[:, cols]), split(inv_ref[cols, :]))
        out_ref[:, cols] = new
        if k + 1 < blocks:
            rest = slice((k + 1) * BLOCK, width)
            out_ref[:, rest] = out_ref[:, rest] - dot3_t(split(new), split(low_ref[rest, cols]))


def solve_rows(gram, low, inv):
    return pl.pallas_call(
        solve_kernel,
        out_shape=jax.ShapeDtypeStruct(gram.shape, jnp.float32),
        in_specs=[pl.BlockSpec(memory_space=pltpu.VMEM)] * 3,
        out_specs=pl.BlockSpec(memory_space=pltpu.VMEM),
        compiler_params=pltpu.CompilerParams(vmem_limit_bytes=24 << 20),
    )(gram, low, inv)


BOTH = ("obs", "unk")
OBS, UNK = 8, 16
CHIPS = UNK // 2
WIDTH = 1024


def add_all(parts):
    total = parts[0]
    for part in parts[1:]:
        total = total + part
    return total


def swap_cores(value):
    return lax.ppermute(value, "unk", [(u, u ^ 1) for u in range(UNK)])


def over_chips(value):
    return [value] + [
        lax.ppermute(value, "unk", [(u, u ^ (2 * k)) for u in range(UNK)]) for k in range(1, CHIPS)
    ]


def from_distance(value, k):
    return lax.ppermute(value, "obs", [(o, o ^ k) for o in range(OBS)])


def high_dot(left, right):
    return lax.dot_general(
        left, right, (((0,), (0,)), ((), ())),
        precision=lax.Precision.HIGH, preferred_element_type=jnp.float32,
    )


def local(design, weights):
    obs, unk = lax.axis_index("obs"), lax.axis_index("unk")
    chip, core = unk // 2, unk % 2
    rows = design.shape[0] // 2

    chunk = jnp.where(unk == 0, design[:, :BLOCK], 0.0)
    for j in range(1, CHIPS):
        pairs = [(o * UNK, o * UNK + 2 * j) for o in range(OBS)]
        chunk = chunk + lax.ppermute(design[:, j * BLOCK : (j + 1) * BLOCK], BOTH, pairs)
    lower = swap_cores(chunk[rows:])
    part = jnp.where(core == 0, chunk[:rows], lower)
    mine = jnp.zeros((rows, WIDTH), jnp.float32)
    for k, got in enumerate(over_chips(part)):
        mine = lax.dynamic_update_slice(mine, got, (0, (chip ^ k) * BLOCK))
    other = swap_cores(mine)
    weighted = design * weights[:, None]
    first = lax.dynamic_slice_in_dim(weighted, core * rows, rows, 0)
    second = lax.dynamic_slice_in_dim(weighted, (1 - core) * rows, rows, 0)
    first_weights = lax.dynamic_slice_in_dim(weights, core * rows, rows, 0)[:, None]
    second_weights = lax.dynamic_slice_in_dim(weights, (1 - core) * rows, rows, 0)[:, None]

    def strips(values, scale):
        low = lax.dynamic_slice_in_dim(values, unk * STRIP, STRIP, 1)
        high = lax.dynamic_slice_in_dim(values, (2 * UNK - 1 - unk) * STRIP, STRIP, 1)
        return jnp.concatenate([low, high], axis=1) * scale

    strip = high_dot(strips(mine, first_weights), mine) + high_dot(strips(other, second_weights), other)
    cut = (unk * STRIP // BLOCK + 1) * BLOCK
    high = jnp.pad(strip[STRIP:], ((0, 0), (WIDTH, BLOCK)))
    high = lax.dynamic_slice_in_dim(high, WIDTH - cut, WIDTH + BLOCK, 1)
    lanes = lax.broadcasted_iota(jnp.int32, high.shape, 1)
    piece = jnp.where(lanes < cut, jnp.pad(strip[:STRIP], ((0, 0), (0, BLOCK))), high)
    partial_value = high_dot(first, mine)
    piece, partial_value, other = lax.optimization_barrier((piece, partial_value, other))
    came = from_distance(piece, 4)
    partial_value = partial_value + high_dot(second, other)
    piece, partial_value = lax.optimization_barrier((piece + came, partial_value))
    came = from_distance(piece, 1)
    owned = partial_value.shape[0] // OBS
    sends = [lax.dynamic_slice_in_dim(partial_value, (obs ^ k) * owned, owned, 0) for k in range(OBS)]
    piece, sends = lax.optimization_barrier((piece + came, sends))
    came = from_distance(piece, 2)
    piece = piece + came
    received = []
    for k in range(1, OBS):
        received.append(from_distance(sends[k], k))
    gathered = over_chips(piece)
    mine_top = jnp.stack(gathered)
    other_top = swap_cores(mine_top)
    where = jnp.stack([chip, core]).astype(jnp.int32)
    low, inverse = cholesky_parts(where, mine_top, other_top)
    owned_rows = add_all([sends[0]] + received)
    return solve_rows(owned_rows, low, inverse)


def solution(mesh):
    return jax.shard_map(
        local,
        mesh=mesh,
        in_specs=(P("obs", "unk"), P("obs")),
        out_specs=P(("unk", "obs"), None),
        check_vma=False,
    )
```

profile of v0, /device:TPU:7, one launch (start us, length us, event | category | flops | bytes accessed | tf_op | source)
XLA Modules:
  0.0 291.5 jit_solution(2037808477354683308)
XLA Ops:
  0.0 2.3 fusion.16
  11.8 2.2 add_add_fusion.1
  14.0 12.6 %collective-permute-start.7 = (f32[512,128]{1,0:T(8,128)S(1)}, f32[512,128]{1,0:T(8,128)S(1)}, u32[]{:S(2)}, u32[]{:S(2)}) collective-permute-start(f32[512,128]{1,0:T(8,128)S(1)} %slice.49), channel_id=1, source_target_pairs={{0,1},{1,0},{2,3},{3,2},{4,5},{5,4},{6,7},{7,6},{8,9},{9,8},{10,11... | collective-permute-start | bytes 786440 | tf_op jit(solution)/shard_map/ppermute | solution.py:197
  28.1 5.6 %collective-permute-start.8 = (f32[512,128]{1,0:T(8,128)S(1)}, f32[512,128]{1,0:T(8,128)S(1)}, u32[]{:S(2)}, u32[]{:S(2)}) collective-permute-start(f32[512,128]{1,0:T(8,128)S(1)} %get-tuple-element.40), channel_id=1, source_target_pairs={{0,2},{1,3},{2,0},{3,1},{4,6},{5,7},{6,4},{7,5},{8,10},{9,11},{10,... | collective-permute-start | bytes 786440 | tf_op jit(solution)/shard_map/ppermute | solution.py:202
  33.7 6.3 %collective-permute-start.9 = (f32[512,128]{1,0:T(8,128)S(1)}, f32[512,128]{1,0:T(8,128)S(1)}, u32[]{:S(2)}, u32[]{:S(2)}) collective-permute-start(f32[512,128]{1,0:T(8,128)S(1)} %get-tuple-element.40), channel_id=1, source_target_pairs={{0,4},{1,5},{2,6},{3,7},{4,0},{5,1},{6,2},{7,3},{8,12},{9,13},{10,... | collective-permute-start | bytes 786440 | tf_op jit(solution)/shard_map/ppermute | solution.py:202
  42.0 2.8 collective-permute-start.13
  44.8 7.1 %collective-permute-done.9 = f32[512,128]{1,0:T(8,128)S(1)} collective-permute-done((f32[512,128]{1,0:T(8,128)S(1)}, f32[512,128]{1,0:T(8,128)S(1)}, u32[]{:S(2)}, u32[]{:S(2)}) %collective-permute-start.9) | collective-permute-done | bytes 262176 | tf_op jit(solution)/shard_map/ppermute | solution.py:202
  54.1 10.3 %collective-permute-done.11 = f32[512,128]{1,0:T(8,128)S(1)} collective-permute-done((f32[512,128]{1,0:T(8,128)S(1)}, f32[512,128]{1,0:T(8,128)S(1)}, u32[]{:S(2)}, u32[]{:S(2)}) %collective-permute-start.11) | collective-permute-done | bytes 262176 | tf_op jit(solution)/shard_map/ppermute | solution.py:202
  66.7 3.3 %broadcast_multiply_fusion = f32[1024,1536]{1,0:T(8,128)S(1)} fusion(f32[1024,1536]{1,0:T(8,128)} %param.2, f32[1024]{0:T(1024)S(1)} %copy-done), kind=kLoop, calls=%fused_computation.4 | loop fusion | flops 1572864 | bytes 12587008 | tf_op jit(solution)/shard_map/mul | solution.py:232
  70.2 5.6 %fusion.2 = f32[1536,1024]{1,0:T(8,128)S(1)} fusion(f32[512,1024]{1,0:T(8,128)S(1)} %constant_dynamic-update-slice_fusion, f32[1024,1536]{1,0:T(8,128)S(1)} %broadcast_multiply_fusion, s32[]{:T(128)S(6)} %select_n.118), kind=kOutput, calls=%fused_computation.2 | convolution fusion | flops 4831838208 | bytes 11534340 | tf_op jit(solution)/shard_map/dot_general | solution.py:211
  77.1 2.5 fusion.6
  80.7 3.6 %collective-permute-start.16 = (f32[32,1152]{1,0:T(8,128)S(1)}, f32[32,1152]{1,0:T(8,128)S(1)}, u32[]{:S(2)}, u32[]{:S(2)}) collective-permute-start(f32[32,1152]{1,0:T(8,128)S(1)} %fusion.9), channel_id=1, source_target_pairs={{0,64},{16,80},{32,96},{48,112},{64,0},{80,16},{96,32},{112,48},{1... | collective-permute-start | bytes 442376 | tf_op jit(solution)/shard_map/ppermute | solution.py:207
  84.2 7.2 %fusion = f32[1536,1024]{1,0:T(8,128)S(1)} fusion(f32[512,1024]{1,0:T(8,128)} %collective-permute-done.15, f32[1024,1536]{1,0:T(8,128)S(1)} %broadcast_multiply_fusion, s32[]{:T(128)S(6)} %select_n.119), kind=kOutput, calls=%fused_computation | convolution fusion | flops 4831838208 | bytes 11534340 | tf_op jit(solution)/shard_map/dot_general | solution.py:211
  91.4 2.2 add.162
  95.6 3.1 %collective-permute-done.17 = f32[32,1152]{1,0:T(8,128)S(1)} collective-permute-done((f32[32,1152]{1,0:T(8,128)S(1)}, f32[32,1152]{1,0:T(8,128)S(1)}, u32[]{:S(2)}, u32[]{:S(2)}) %collective-permute-start.17) | collective-permute-done | bytes 147488 | tf_op jit(solution)/shard_map/ppermute | solution.py:207
  98.8 3.0 %collective-permute-start.25 = (f32[32,1152]{1,0:T(8,128)S(1)}, f32[32,1152]{1,0:T(8,128)S(1)}, u32[]{:S(2)}, u32[]{:S(2)}) collective-permute-start(f32[32,1152]{1,0:T(8,128)S(1)} %add.163), channel_id=1, source_target_pairs={{0,32},{16,48},{32,0},{48,16},{64,96},{80,112},{96,64},{112,80},{1... | collective-permute-start | bytes 442376 | tf_op jit(solution)/shard_map/ppermute | solution.py:207
  101.8 2.6 collective-permute-done.25
  106.5 3.2 %collective-permute-start.24 = (f32[192,1024]{1,0:T(8,128)S(1)}, f32[192,1024]{1,0:T(8,128)S(1)}, u32[]{:S(2)}, u32[]{:S(2)}) collective-permute-start(f32[192,1024]{1,0:T(8,128)S(1)} %get-tuple-element.33), channel_id=1, source_target_pairs={{0,112},{16,96},{32,80},{48,64},{64,48},{80,32},{96,16},{112,0},{1... | collective-permute-start | bytes 2359304 | tf_op jit(solution)/shard_map/ppermute | solution.py:207
  109.7 2.3 collective-permute-start.23
  112.6 2.2 collective-permute-start.21
  116.6 4.0 %collective-permute-done.27 = f32[32,1152]{1,0:T(8,128)S(1)} collective-permute-done((f32[32,1152]{1,0:T(8,128)S(1)}, f32[32,1152]{1,0:T(8,128)S(1)}, u32[]{:S(2)}, u32[]{:S(2)}) %collective-permute-start.27) | collective-permute-done | bytes 147488 | tf_op jit(solution)/shard_map/ppermute | solution.py:202
  121.3 5.1 %collective-permute-done.28 = f32[32,1152]{1,0:T(8,128)S(1)} collective-permute-done((f32[32,1152]{1,0:T(8,128)S(1)}, f32[32,1152]{1,0:T(8,128)S(1)}, u32[]{:S(2)}, u32[]{:S(2)}) %collective-permute-start.28) | collective-permute-done | bytes 147488 | tf_op jit(solution)/shard_map/ppermute | solution.py:202
  126.5 2.5 collective-permute-start.29
  129.0 54.2 %collective-permute-done.29 = f32[32,1152]{1,0:T(8,128)S(1)} collective-permute-done((f32[32,1152]{1,0:T(8,128)S(1)}, f32[32,1152]{1,0:T(8,128)S(1)}, u32[]{:S(2)}, u32[]{:S(2)}) %collective-permute-start.29) | collective-permute-done | bytes 147488 | tf_op jit(solution)/shard_map/ppermute | solution.py:202
  183.2 5.8 %collective-permute-done.30 = f32[32,1152]{1,0:T(8,128)S(1)} collective-permute-done((f32[32,1152]{1,0:T(8,128)S(1)}, f32[32,1152]{1,0:T(8,128)S(1)}, u32[]{:S(2)}, u32[]{:S(2)}) %collective-permute-start.30) | collective-permute-done | bytes 147488 | tf_op jit(solution)/shard_map/ppermute | solution.py:202
  189.9 5.5 %collective-permute-done.31 = f32[32,1152]{1,0:T(8,128)S(1)} collective-permute-done((f32[32,1152]{1,0:T(8,128)S(1)}, f32[32,1152]{1,0:T(8,128)S(1)}, u32[]{:S(2)}, u32[]{:S(2)}) %collective-permute-start.31) | collective-permute-done | bytes 147488 | tf_op jit(solution)/shard_map/ppermute | solution.py:202
  195.4 6.1 %collective-permute-done.32 = f32[32,1152]{1,0:T(8,128)S(1)} collective-permute-done((f32[32,1152]{1,0:T(8,128)S(1)}, f32[32,1152]{1,0:T(8,128)S(1)}, u32[]{:S(2)}, u32[]{:S(2)}) %collective-permute-start.32) | collective-permute-done | bytes 147488 | tf_op jit(solution)/shard_map/ppermute | solution.py:202
  201.5 2.7 collective-permute-start.20
  204.8 4.6 %collective-permute-start.33 = (f32[8,32,1152]{2,1,0:T(8,128)S(1)}, f32[8,32,1152]{2,1,0:T(8,128)S(1)}, u32[]{:S(2)}, u32[]{:S(2)}) collective-permute-start(f32[8,32,1152]{2,1,0:T(8,128)S(1)} %bitcast_dynamic-update-slice_fusion.mine_ref), channel_id=1, source_target_pairs={{0,1},{1,0},{2,3},{3,2},{4,5},{5,4},{6,7},{7,6},{8,9},{9,8},{10,11... | collective-permute-start | bytes 3538952 | tf_op jit(solution)/shard_map/ppermute | solution.py:197
  209.4 28.5 %collective-permute-done.20 = f32[192,1024]{1,0:T(8,128)S(1)} collective-permute-done((f32[192,1024]{1,0:T(8,128)S(1)}, f32[192,1024]{1,0:T(8,128)S(1)}, u32[]{:S(2)}, u32[]{:S(2)}) %collective-permute-start.20) | collective-permute-done | bytes 786464 | tf_op jit(solution)/shard_map/ppermute | solution.py:207
  238.6 48.2 %shard_map.28 = (f32[1024,1024]{1,0:T(8,128)S(1)}, f32[1024,128]{1,0:T(8,128)S(1)}) custom-call(s32[2]{0:T(128)S(1)} %pad_add_fusion.where_ref, f32[8,32,1152]{2,1,0:T(8,128)S(1)} %bitcast_dynamic-update-slice_fusion.mine_ref, f32[8,32,1152]{2,1,0:T(8,128)S(1)} %collective-permute-done.33.other_ref), custom_call_target="tpu_custom_call" | custom-call | flops 80000000000 | bytes 8388608 | tf_op jit(solution)/shard_map/pallas_call | solution.py:137
  286.9 4.6 %shard_map.29 = f32[192,1024]{1,0:T(8,128)} custom-call(f32[192,1024]{1,0:T(8,128)S(1)} %add_add_fusion.gram_ref, f32[1024,1024]{1,0:T(8,128)S(1)} %get-tuple-element.35.low_ref, f32[1024,128]{1,0:T(8,128)S(1)} %get-tuple-element.36.inv_ref), custom_call_target="tpu_custom_call" | custom-call | tf_op jit(solution)/shard_map/pallas_call | solution.py:174
  (77 shorter events, 29.4 us)
Async XLA Ops:
  2.3 6.5 %collective-permute-start.6 = (f32[1024,128]{1,0:T(8,128)S(1)}, f32[1024,128]{1,0:T(8,128)S(1)}, u32[]{:S(2)}, u32[]{:S(2)}) collective-permute-start(f32[1024,128]{1,0:T(8,128)S(1)} %get-tuple-element.55), channel_id=1, source_target_pairs={{0,14},{16,30},{32,46},{48,62},{64,78},{80,94},{96,110},{112,126}} | collective-permute-start | bytes 1572872 | tf_op jit(solution)/shard_map/ppermute | solution.py:225
  3.0 7.3 %collective-permute-start.5 = (f32[1024,128]{1,0:T(8,128)S(1)}, f32[1024,128]{1,0:T(8,128)}, u32[]{:S(2)}, u32[]{:S(2)}) collective-permute-start(f32[1024,128]{1,0:T(8,128)S(1)} %get-tuple-element.50), channel_id=1, source_target_pairs={{0,12},{16,28},{32,44},{48,60},{64,76},{80,92},{96,108},{112,124}} | collective-permute-start | bytes 1572872 | tf_op jit(solution)/shard_map/ppermute | solution.py:225
  4.5 7.3 %collective-permute-start.4 = (f32[1024,128]{1,0:T(8,128)S(1)}, f32[1024,128]{1,0:T(8,128)}, u32[]{:S(2)}, u32[]{:S(2)}) collective-permute-start(f32[1024,128]{1,0:T(8,128)S(1)} %get-tuple-element.51), channel_id=1, source_target_pairs={{0,10},{16,26},{32,42},{48,58},{64,74},{80,90},{96,106},{112,122}} | collective-permute-start | bytes 1572872 | tf_op jit(solution)/shard_map/ppermute | solution.py:225
  5.9 5.9 %collective-permute-start.3 = (f32[1024,128]{1,0:T(8,128)S(1)}, f32[1024,128]{1,0:T(8,128)}, u32[]{:S(2)}, u32[]{:S(2)}) collective-permute-start(f32[1024,128]{1,0:T(8,128)S(1)} %get-tuple-element.52), channel_id=1, source_target_pairs={{0,8},{16,24},{32,40},{48,56},{64,72},{80,88},{96,104},{112,120}} | collective-permute-start | bytes 1572872 | tf_op jit(solution)/shard_map/ppermute | solution.py:225
  7.4 4.4 %collective-permute-start.2 = (f32[1024,128]{1,0:T(8,128)S(1)}, f32[1024,128]{1,0:T(8,128)}, u32[]{:S(2)}, u32[]{:S(2)}) collective-permute-start(f32[1024,128]{1,0:T(8,128)S(1)} %get-tuple-element.53), channel_id=1, source_target_pairs={{0,6},{16,22},{32,38},{48,54},{64,70},{80,86},{96,102},{112,118}} | collective-permute-start | bytes 1572872 | tf_op jit(solution)/shard_map/ppermute | solution.py:225
  14.0 13.7 %collective-permute-start.7 = (f32[512,128]{1,0:T(8,128)S(1)}, f32[512,128]{1,0:T(8,128)S(1)}, u32[]{:S(2)}, u32[]{:S(2)}) collective-permute-start(f32[512,128]{1,0:T(8,128)S(1)} %slice.49), channel_id=1, source_target_pairs={{0,1},{1,0},{2,3},{3,2},{4,5},{5,4},{6,7},{7,6},{8,9},{9,8},{10,11... | collective-permute-start | bytes 786440 | tf_op jit(solution)/shard_map/ppermute | solution.py:197
  28.1 13.9 %collective-permute-start.8 = (f32[512,128]{1,0:T(8,128)S(1)}, f32[512,128]{1,0:T(8,128)S(1)}, u32[]{:S(2)}, u32[]{:S(2)}) collective-permute-start(f32[512,128]{1,0:T(8,128)S(1)} %get-tuple-element.40), channel_id=1, source_target_pairs={{0,2},{1,3},{2,0},{3,1},{4,6},{5,7},{6,4},{7,5},{8,10},{9,11},{10,... | collective-permute-start | bytes 786440 | tf_op jit(solution)/shard_map/ppermute | solution.py:202
  33.7 18.2 %collective-permute-start.9 = (f32[512,128]{1,0:T(8,128)S(1)}, f32[512,128]{1,0:T(8,128)S(1)}, u32[]{:S(2)}, u32[]{:S(2)}) collective-permute-start(f32[512,128]{1,0:T(8,128)S(1)} %get-tuple-element.40), channel_id=1, source_target_pairs={{0,4},{1,5},{2,6},{3,7},{4,0},{5,1},{6,2},{7,3},{8,12},{9,13},{10,... | collective-permute-start | bytes 786440 | tf_op jit(solution)/shard_map/ppermute | solution.py:202
  40.0 14.0 %collective-permute-start.10 = (f32[512,128]{1,0:T(8,128)S(1)}, f32[512,128]{1,0:T(8,128)S(1)}, u32[]{:S(2)}, u32[]{:S(2)}) collective-permute-start(f32[512,128]{1,0:T(8,128)S(1)} %get-tuple-element.40), channel_id=1, source_target_pairs={{0,6},{1,7},{2,4},{3,5},{4,2},{5,3},{6,0},{7,1},{8,14},{9,15},{10,... | collective-permute-start | bytes 786440 | tf_op jit(solution)/shard_map/ppermute | solution.py:202
  40.2 24.2 %collective-permute-start.11 = (f32[512,128]{1,0:T(8,128)S(1)}, f32[512,128]{1,0:T(8,128)S(1)}, u32[]{:S(2)}, u32[]{:S(2)}) collective-permute-start(f32[512,128]{1,0:T(8,128)S(1)} %get-tuple-element.40), channel_id=1, source_target_pairs={{0,8},{1,9},{2,10},{3,11},{4,12},{5,13},{6,14},{7,15},{8,0},{9,1},... | collective-permute-start | bytes 786440 | tf_op jit(solution)/shard_map/ppermute | solution.py:202
  40.2 24.2 %collective-permute-start.12 = (f32[512,128]{1,0:T(8,128)S(1)}, f32[512,128]{1,0:T(8,128)S(1)}, u32[]{:S(2)}, u32[]{:S(2)}) collective-permute-start(f32[512,128]{1,0:T(8,128)S(1)} %get-tuple-element.40), channel_id=1, source_target_pairs={{0,10},{1,11},{2,8},{3,9},{4,14},{5,15},{6,12},{7,13},{8,2},{9,3},... | collective-permute-start | bytes 786440 | tf_op jit(solution)/shard_map/ppermute | solution.py:202
  42.0 22.5 %collective-permute-start.13 = (f32[512,128]{1,0:T(8,128)S(1)}, f32[512,128]{1,0:T(8,128)S(1)}, u32[]{:S(2)}, u32[]{:S(2)}) collective-permute-start(f32[512,128]{1,0:T(8,128)S(1)} %get-tuple-element.40), channel_id=1, source_target_pairs={{0,12},{1,13},{2,14},{3,15},{4,8},{5,9},{6,10},{7,11},{8,4},{9,5},... | collective-permute-start | bytes 786440 | tf_op jit(solution)/shard_map/ppermute | solution.py:202
  51.9 13.8 %collective-permute-start.14 = (f32[512,128]{1,0:T(8,128)S(1)}, f32[512,128]{1,0:T(8,128)S(1)}, u32[]{:S(2)}, u32[]{:S(2)}) collective-permute-start(f32[512,128]{1,0:T(8,128)S(1)} %get-tuple-element.40), channel_id=1, source_target_pairs={{0,14},{1,15},{2,12},{3,13},{4,10},{5,11},{6,8},{7,9},{8,6},{9,7},... | collective-permute-start | bytes 786440 | tf_op jit(solution)/shard_map/ppermute | solution.py:202
  65.7 10.1 %collective-permute-start.15 = (f32[512,1024]{1,0:T(8,128)S(1)}, f32[512,1024]{1,0:T(8,128)}, u32[]{:S(2)}, u32[]{:S(2)}) collective-permute-start(f32[512,1024]{1,0:T(8,128)S(1)} %constant_dynamic-update-slice_fusion), channel_id=1, source_target_pairs={{0,1},{1,0},{2,3},{3,2},{4,5},{5,4},{6,7},{7,6},{8,9},{9,8},{10,11... | collective-permute-start | bytes 6291464 | tf_op jit(solution)/shard_map/ppermute | solution.py:197
  80.7 12.9 %collective-permute-start.16 = (f32[32,1152]{1,0:T(8,128)S(1)}, f32[32,1152]{1,0:T(8,128)S(1)}, u32[]{:S(2)}, u32[]{:S(2)}) collective-permute-start(f32[32,1152]{1,0:T(8,128)S(1)} %fusion.9), channel_id=1, source_target_pairs={{0,64},{16,80},{32,96},{48,112},{64,0},{80,16},{96,32},{112,48},{1... | collective-permute-start | bytes 442376 | tf_op jit(solution)/shard_map/ppermute | solution.py:207
  93.7 5.1 %collective-permute-start.17 = (f32[32,1152]{1,0:T(8,128)S(1)}, f32[32,1152]{1,0:T(8,128)S(1)}, u32[]{:S(2)}, u32[]{:S(2)}) collective-permute-start(f32[32,1152]{1,0:T(8,128)S(1)} %add.161), channel_id=1, source_target_pairs={{0,16},{16,0},{32,48},{48,32},{64,80},{80,64},{96,112},{112,96},{1... | collective-permute-start | bytes 442376 | tf_op jit(solution)/shard_map/ppermute | solution.py:207
  98.8 5.6 %collective-permute-start.25 = (f32[32,1152]{1,0:T(8,128)S(1)}, f32[32,1152]{1,0:T(8,128)S(1)}, u32[]{:S(2)}, u32[]{:S(2)}) collective-permute-start(f32[32,1152]{1,0:T(8,128)S(1)} %add.163), channel_id=1, source_target_pairs={{0,32},{16,48},{32,0},{48,16},{64,96},{80,112},{96,64},{112,80},{1... | collective-permute-start | bytes 442376 | tf_op jit(solution)/shard_map/ppermute | solution.py:207
  104.4 10.4 %collective-permute-start.26 = (f32[32,1152]{1,0:T(8,128)S(1)}, f32[32,1152]{1,0:T(8,128)S(1)}, u32[]{:S(2)}, u32[]{:S(2)}) collective-permute-start(f32[32,1152]{1,0:T(8,128)S(1)} %get-tuple-element.38), channel_id=1, source_target_pairs={{0,2},{1,3},{2,0},{3,1},{4,6},{5,7},{6,4},{7,5},{8,10},{9,11},{10,... | collective-permute-start | bytes 442376 | tf_op jit(solution)/shard_map/ppermute | solution.py:202
  106.5 97.7 %collective-permute-start.24 = (f32[192,1024]{1,0:T(8,128)S(1)}, f32[192,1024]{1,0:T(8,128)S(1)}, u32[]{:S(2)}, u32[]{:S(2)}) collective-permute-start(f32[192,1024]{1,0:T(8,128)S(1)} %get-tuple-element.33), channel_id=1, source_target_pairs={{0,112},{16,96},{32,80},{48,64},{64,48},{80,32},{96,16},{112,0},{1... | collective-permute-start | bytes 2359304 | tf_op jit(solution)/shard_map/ppermute | solution.py:207
  109.7 94.5 %collective-permute-start.23 = (f32[192,1024]{1,0:T(8,128)S(1)}, f32[192,1024]{1,0:T(8,128)S(1)}, u32[]{:S(2)}, u32[]{:S(2)}) collective-permute-start(f32[192,1024]{1,0:T(8,128)S(1)} %get-tuple-element.32), channel_id=1, source_target_pairs={{0,96},{16,112},{32,64},{48,80},{64,32},{80,48},{96,0},{112,16},{1... | collective-permute-start | bytes 2359304 | tf_op jit(solution)/shard_map/ppermute | solution.py:207
  112.0 92.8 %collective-permute-start.22 = (f32[192,1024]{1,0:T(8,128)S(1)}, f32[192,1024]{1,0:T(8,128)S(1)}, u32[]{:S(2)}, u32[]{:S(2)}) collective-permute-start(f32[192,1024]{1,0:T(8,128)S(1)} %get-tuple-element.31), channel_id=1, source_target_pairs={{0,80},{16,64},{32,112},{48,96},{64,16},{80,0},{96,48},{112,32},{1... | collective-permute-start | bytes 2359304 | tf_op jit(solution)/shard_map/ppermute | solution.py:207
  112.6 96.8 %collective-permute-start.21 = (f32[192,1024]{1,0:T(8,128)S(1)}, f32[192,1024]{1,0:T(8,128)S(1)}, u32[]{:S(2)}, u32[]{:S(2)}) collective-permute-start(f32[192,1024]{1,0:T(8,128)S(1)} %get-tuple-element.30), channel_id=1, source_target_pairs={{0,64},{16,80},{32,96},{48,112},{64,0},{80,16},{96,32},{112,48},{1... | collective-permute-start | bytes 2359304 | tf_op jit(solution)/shard_map/ppermute | solution.py:207
  114.8 5.8 %collective-permute-start.27 = (f32[32,1152]{1,0:T(8,128)S(1)}, f32[32,1152]{1,0:T(8,128)S(1)}, u32[]{:S(2)}, u32[]{:S(2)}) collective-permute-start(f32[32,1152]{1,0:T(8,128)S(1)} %get-tuple-element.38), channel_id=1, source_target_pairs={{0,4},{1,5},{2,6},{3,7},{4,0},{5,1},{6,2},{7,3},{8,12},{9,13},{10,... | collective-permute-start | bytes 442376 | tf_op jit(solution)/shard_map/ppermute | solution.py:202
  120.6 5.8 %collective-permute-start.28 = (f32[32,1152]{1,0:T(8,128)S(1)}, f32[32,1152]{1,0:T(8,128)S(1)}, u32[]{:S(2)}, u32[]{:S(2)}) collective-permute-start(f32[32,1152]{1,0:T(8,128)S(1)} %get-tuple-element.38), channel_id=1, source_target_pairs={{0,6},{1,7},{2,4},{3,5},{4,2},{5,3},{6,0},{7,1},{8,14},{9,15},{10,... | collective-permute-start | bytes 442376 | tf_op jit(solution)/shard_map/ppermute | solution.py:202
  126.5 56.7 %collective-permute-start.29 = (f32[32,1152]{1,0:T(8,128)S(1)}, f32[32,1152]{1,0:T(8,128)S(1)}, u32[]{:S(2)}, u32[]{:S(2)}) collective-permute-start(f32[32,1152]{1,0:T(8,128)S(1)} %get-tuple-element.38), channel_id=1, source_target_pairs={{0,8},{1,9},{2,10},{3,11},{4,12},{5,13},{6,14},{7,15},{8,0},{9,1},... | collective-permute-start | bytes 442376 | tf_op jit(solution)/shard_map/ppermute | solution.py:202
  183.2 5.8 %collective-permute-start.30 = (f32[32,1152]{1,0:T(8,128)S(1)}, f32[32,1152]{1,0:T(8,128)S(1)}, u32[]{:S(2)}, u32[]{:S(2)}) collective-permute-start(f32[32,1152]{1,0:T(8,128)S(1)} %get-tuple-element.38), channel_id=1, source_target_pairs={{0,10},{1,11},{2,8},{3,9},{4,14},{5,15},{6,12},{7,13},{8,2},{9,3},... | collective-permute-start | bytes 442376 | tf_op jit(solution)/shard_map/ppermute | solution.py:202
  189.0 6.4 %collective-permute-start.31 = (f32[32,1152]{1,0:T(8,128)S(1)}, f32[32,1152]{1,0:T(8,128)S(1)}, u32[]{:S(2)}, u32[]{:S(2)}) collective-permute-start(f32[32,1152]{1,0:T(8,128)S(1)} %get-tuple-element.38), channel_id=1, source_target_pairs={{0,12},{1,13},{2,14},{3,15},{4,8},{5,9},{6,10},{7,11},{8,4},{9,5},... | collective-permute-start | bytes 442376 | tf_op jit(solution)/shard_map/ppermute | solution.py:202
  195.4 6.1 %collective-permute-start.32 = (f32[32,1152]{1,0:T(8,128)S(1)}, f32[32,1152]{1,0:T(8,128)S(1)}, u32[]{:S(2)}, u32[]{:S(2)}) collective-permute-start(f32[32,1152]{1,0:T(8,128)S(1)} %get-tuple-element.38), channel_id=1, source_target_pairs={{0,14},{1,15},{2,12},{3,13},{4,10},{5,11},{6,8},{7,9},{8,6},{9,7},... | collective-permute-start | bytes 442376 | tf_op jit(solution)/shard_map/ppermute | solution.py:202
  201.5 36.4 %collective-permute-start.20 = (f32[192,1024]{1,0:T(8,128)S(1)}, f32[192,1024]{1,0:T(8,128)S(1)}, u32[]{:S(2)}, u32[]{:S(2)}) collective-permute-start(f32[192,1024]{1,0:T(8,128)S(1)} %get-tuple-element.29), channel_id=1, source_target_pairs={{0,48},{16,32},{32,16},{48,0},{64,112},{80,96},{96,80},{112,64},{1... | collective-permute-start | bytes 2359304 | tf_op jit(solution)/shard_map/ppermute | solution.py:207
  204.2 33.8 %collective-permute-start.19 = (f32[192,1024]{1,0:T(8,128)S(1)}, f32[192,1024]{1,0:T(8,128)S(1)}, u32[]{:S(2)}, u32[]{:S(2)}) collective-permute-start(f32[192,1024]{1,0:T(8,128)S(1)} %get-tuple-element.28), channel_id=1, source_target_pairs={{0,32},{16,48},{32,0},{48,16},{64,96},{80,112},{96,64},{112,80},{1... | collective-permute-start | bytes 2359304 | tf_op jit(solution)/shard_map/ppermute | solution.py:207
  204.2 33.8 %collective-permute-start.18 = (f32[192,1024]{1,0:T(8,128)S(1)}, f32[192,1024]{1,0:T(8,128)S(1)}, u32[]{:S(2)}, u32[]{:S(2)}) collective-permute-start(f32[192,1024]{1,0:T(8,128)S(1)} %get-tuple-element.27), channel_id=1, source_target_pairs={{0,16},{16,0},{32,48},{48,32},{64,80},{80,64},{96,112},{112,96},{1... | collective-permute-start | bytes 2359304 | tf_op jit(solution)/shard_map/ppermute | solution.py:207
  204.8 33.9 %collective-permute-start.33 = (f32[8,32,1152]{2,1,0:T(8,128)S(1)}, f32[8,32,1152]{2,1,0:T(8,128)S(1)}, u32[]{:S(2)}, u32[]{:S(2)}) collective-permute-start(f32[8,32,1152]{2,1,0:T(8,128)S(1)} %bitcast_dynamic-update-slice_fusion.mine_ref), channel_id=1, source_target_pairs={{0,1},{1,0},{2,3},{3,2},{4,5},{5,4},{6,7},{7,6},{8,9},{9,8},{10,11... | collective-permute-start | bytes 3538952 | tf_op jit(solution)/shard_map/ppermute | solution.py:197
  (3 other events, 43.0 us)
where the time goes:
time: 294 us; the launch traced here: 291 us
  waiting for transfers between devices  137 us (47%)
  starting transfers between devices  71.8 us (24%)
  Pallas kernels  52.8 us (18%)
  matrix products  16.3 us (6%)
  other arithmetic  8.51 us (3%)
  local copies, waits for them, and re-layouts  4.94 us (2%)
    ppermute x14, waiting for transfers between devices, over_chips(): lax.ppermute(value, 'unk', [(u, u ^ 2 * k) for u in range(UNK)])  101 us
    pallas_call x1, Pallas kernels, cholesky_parts(): pl.pallas_call(chol_kernel, out_shape=(jax.ShapeDtypeStruct((width, width...  48.2 us
    ppermute x10, waiting for transfers between devices, from_distance(): return lax.ppermute(value, 'obs', [(o, o ^ k) for o in range(OBS)])  34.2 us
    ppermute x14, starting transfers between devices, over_chips(): lax.ppermute(value, 'unk', [(u, u ^ 2 * k) for u in range(UNK)])  24.7 us
    ppermute x10, starting transfers between devices, from_distance(): return lax.ppermute(value, 'obs', [(o, o ^ k) for o in range(OBS)])  19.5 us
    ppermute x3, starting transfers between devices, swap_cores(): return lax.ppermute(value, 'unk', [(u, u ^ 1) for u in range(UNK)])  18 us
    dot_general x4, matrix products, high_dot(): lax.dot_general(left, right, (((0,), (0,)), ((), ())), precision=lax.Prec...  16.3 us
    ppermute x7, starting transfers between devices, local(): lax.ppermute(design[:, j * BLOCK:(j + 1) * BLOCK], BOTH, pairs)  9.46 us
  transfers between devices with their start and end apart: 34, of which 14 were waited for; matrix products, arithmetic and copies ran while one was open for 7% of the time, Pallas kernels for 0%

commit v1 on v0

--- a/solution.py
+++ b/solution.py
@@ -6,7 +6,7 @@
 
 BLOCK = 128
 SUB = 8
-STRIP = 32
+STRIP = 64
 
 
 def split(x):
@@ -132,7 +132,7 @@
 
 def cholesky_parts(where, mine, other):
     count, strip, packed = mine.shape
-    width = count * BLOCK
+    width = 4 * count * strip
     vmem = pl.BlockSpec(memory_space=pltpu.VMEM)
     return pl.pallas_call(
         chol_kernel,
@@ -183,6 +183,8 @@
 BOTH = ("obs", "unk")
 OBS, UNK = 8, 16
 CHIPS = UNK // 2
+LINE = 4
+STRIPS = 2 * LINE
 WIDTH = 1024
 
 
@@ -197,9 +199,9 @@
     return lax.ppermute(value, "unk", [(u, u ^ 1) for u in range(UNK)])
 
 
-def over_chips(value):
+def over_chips(value, chips):
     return [value] + [
-        lax.ppermute(value, "unk", [(u, u ^ (2 * k)) for u in range(UNK)]) for k in range(1, CHIPS)
+        lax.ppermute(value, "unk", [(u, u ^ (2 * k)) for u in range(UNK)]) for k in range(1, chips)
     ]
 
 
@@ -223,35 +225,40 @@
     for j in range(1, CHIPS):
         pairs = [(o * UNK, o * UNK + 2 * j) for o in range(OBS)]
         chunk = chunk + lax.ppermute(design[:, j * BLOCK : (j + 1) * BLOCK], BOTH, pairs)
+    weighted = design * weights[:, None]
+    chunk, weighted = lax.optimization_barrier((chunk, weighted))
     lower = swap_cores(chunk[rows:])
     part = jnp.where(core == 0, chunk[:rows], lower)
     mine = jnp.zeros((rows, WIDTH), jnp.float32)
-    for k, got in enumerate(over_chips(part)):
+    for k, got in enumerate(over_chips(part, CHIPS)):
         mine = lax.dynamic_update_slice(mine, got, (0, (chip ^ k) * BLOCK))
     other = swap_cores(mine)
-    weighted = design * weights[:, None]
     first = lax.dynamic_slice_in_dim(weighted, core * rows, rows, 0)
     second = lax.dynamic_slice_in_dim(weighted, (1 - core) * rows, rows, 0)
     first_weights = lax.dynamic_slice_in_dim(weights, core * rows, rows, 0)[:, None]
     second_weights = lax.dynamic_slice_in_dim(weights, (1 - core) * rows, rows, 0)[:, None]
 
+    spot = chip % LINE * 2 + core
+
     def strips(values, scale):
-        low = lax.dynamic_slice_in_dim(values, unk * STRIP, STRIP, 1)
-        high = lax.dynamic_slice_in_dim(values, (2 * UNK - 1 - unk) * STRIP, STRIP, 1)
+        low = lax.dynamic_slice_in_dim(values, spot * STRIP, STRIP, 1)
+        high = lax.dynamic_slice_in_dim(values, (2 * STRIPS - 1 - spot) * STRIP, STRIP, 1)
         return jnp.concatenate([low, high], axis=1) * scale
 
-    strip = high_dot(strips(mine, first_weights), mine) + high_dot(strips(other, second_weights), other)
-    cut = (unk * STRIP // BLOCK + 1) * BLOCK
+    strip = high_dot(strips(mine, first_weights), mine)
+    strip, other = lax.optimization_barrier((strip, other))
+    strip = strip + high_dot(strips(other, second_weights), other)
+    cut = (spot * STRIP // BLOCK + 1) * BLOCK
     high = jnp.pad(strip[STRIP:], ((0, 0), (WIDTH, BLOCK)))
     high = lax.dynamic_slice_in_dim(high, WIDTH - cut, WIDTH + BLOCK, 1)
     lanes = lax.broadcasted_iota(jnp.int32, high.shape, 1)
     piece = jnp.where(lanes < cut, jnp.pad(strip[:STRIP], ((0, 0), (0, BLOCK))), high)
+    piece, mine, other = lax.optimization_barrier((piece, mine, other))
+    came = from_distance(piece, 4)
     partial_value = high_dot(first, mine)
-    piece, partial_value, other = lax.optimization_barrier((piece, partial_value, other))
-    came = from_distance(piece, 4)
+    piece, partial_value, other = lax.optimization_barrier((piece + came, partial_value, other))
+    came = from_distance(piece, 1)
     partial_value = partial_value + high_dot(second, other)
-    piece, partial_value = lax.optimization_barrier((piece + came, partial_value))
-    came = from_distance(piece, 1)
     owned = partial_value.shape[0] // OBS
     sends = [lax.dynamic_slice_in_dim(partial_value, (obs ^ k) * owned, owned, 0) for k in range(OBS)]
     piece, sends = lax.optimization_barrier((piece + came, sends))
@@ -260,10 +267,10 @@
     received = []
     for k in range(1, OBS):
         received.append(from_distance(sends[k], k))
-    gathered = over_chips(piece)
+    gathered = over_chips(piece, LINE)
     mine_top = jnp.stack(gathered)
     other_top = swap_cores(mine_top)
-    where = jnp.stack([chip, core]).astype(jnp.int32)
+    where = jnp.stack([chip % LINE, core]).astype(jnp.int32)
     low, inverse = cholesky_parts(where, mine_top, other_top)
     owned_rows = add_all([sends[0]] + received)
     return solve_rows(owned_rows, low, inverse)

time: 294 us -> 258 us (0.88)
  waiting for transfers between devices: 137 us -> 93.2 us
  starting transfers between devices: 71.8 us -> 62.2 us
  local copies, waits for them, and re-layouts: 4.94 us -> 13.4 us
  other arithmetic: 8.51 us -> 13 us
    ppermute x14 -> x10, waiting for transfers between devices: 101 us -> 26.9 us  [over_chips(): lax.ppermute(value, 'unk', [(u, u ^ 2 * k) for u in range(UNK)])]
    ppermute x10, waiting for transfers between devices: 34.2 us -> 64.8 us  [from_distance(): return lax.ppermute(value, 'obs', [(o, o ^ k) for o in range(OBS)])]
    ppermute x14 -> x10, starting transfers between devices: 24.7 us -> 18.9 us  [over_chips(): lax.ppermute(value, 'unk', [(u, u ^ 2 * k) for u in range(UNK)])]
    ppermute x3, starting transfers between devices: 18 us -> 12.6 us  [swap_cores(): return lax.ppermute(value, 'unk', [(u, u ^ 1) for u in range(UNK)])]
    dynamic_update_slice x7, local copies, waits for them, and re-layouts: 0.17 us -> 5.35 us  [local(): mine = lax.dynamic_update_slice(mine, got, (0, (chip ^ k) * BLOCK))]
  transfers between devices with their start and end apart: 34 -> 30, of which waited for: 14 -> 13; matrix products, arithmetic and copies ran while one was open for 7% -> 13% of each run, Pallas kernels for 0% -> 0%
where the time goes in v1:
time: 258 us; the launch traced here: 254 us
  waiting for transfers between devices  93.2 us (36%)
  starting transfers between devices  62.2 us (24%)
  Pallas kernels  52.8 us (20%)
  matrix products  19.2 us (7%)
  local copies, waits for them, and re-layouts  13.4 us (5%)
  other arithmetic  13 us (5%)
    ppermute x10, waiting for transfers between devices, from_distance(): return lax.ppermute(value, 'obs', [(o, o ^ k) for o in range(OBS)])  64.8 us
    pallas_call x1, Pallas kernels, cholesky_parts(): pl.pallas_call(chol_kernel, out_shape=(jax.ShapeDtypeStruct((width, width...  48.3 us
    ppermute x10, waiting for transfers between devices, over_chips(): lax.ppermute(value, 'unk', [(u, u ^ 2 * k) for u in range(UNK)])  26.9 us
    ppermute x10, starting transfers between devices, from_distance(): return lax.ppermute(value, 'obs', [(o, o ^ k) for o in range(OBS)])  21.9 us
    dot_general x4, matrix products, high_dot(): lax.dot_general(left, right, (((0,), (0,)), ((), ())), precision=lax.Prec...  19.2 us
    ppermute x10, starting transfers between devices, over_chips(): lax.ppermute(value, 'unk', [(u, u ^ 2 * k) for u in range(UNK)])  18.9 us
    ppermute x3, starting transfers between devices, swap_cores(): return lax.ppermute(value, 'unk', [(u, u ^ 1) for u in range(UNK)])  12.6 us
    ppermute x7, starting transfers between devices, local(): lax.ppermute(design[:, j * BLOCK:(j + 1) * BLOCK], BOTH, pairs)  8.81 us
  transfers between devices with their start and end apart: 30, of which 13 were waited for; matrix products, arithmetic and copies ran while one was open for 13% of the time, Pallas kernels for 0%

profile of v1, /device:TPU:7, one launch (start us, length us, event | category | flops | bytes accessed | tf_op | source)
XLA Modules:
  0.0 254.1 jit_solution(3821588541909578302)
XLA Ops:
  0.0 3.1 %fusion.17 = (f32[1024,128]{1,0:T(8,128)S(1)}, f32[1024,128]{1,0:T(8,128)S(1)}, f32[1024,128]{1,0:T(8,128)S(1)}, f32[1024,128]{1,0:T(8,128)S(1)}, f32[1024,128]{...) fusion(f32[1024,1536]{1,0:T(8,128)} %param.2), kind=kLoop, calls=%fused_computation.47 | loop fusion | bytes 7340032 | tf_op jit(solution)/shard_map/slice | solution.py:227
  12.0 5.9 %broadcast_multiply_fusion = f32[1024,1536]{1,0:T(8,128)} fusion(f32[1024,1536]{1,0:T(8,128)} %param.2, f32[1024]{0:T(1024)S(1)} %copy-done), kind=kLoop, calls=%fused_computation.4 | loop fusion | flops 1572864 | bytes 12587008 | tf_op jit(solution)/shard_map/mul | solution.py:228
  17.9 2.1 add_add_fusion.1
  20.1 8.1 %collective-permute-start.7 = (f32[512,128]{1,0:T(8,128)S(1)}, f32[512,128]{1,0:T(8,128)S(1)}, u32[]{:S(2)}, u32[]{:S(2)}) collective-permute-start(f32[512,128]{1,0:T(8,128)S(1)} %slice.45), channel_id=1, source_target_pairs={{0,1},{1,0},{2,3},{3,2},{4,5},{5,4},{6,7},{7,6},{8,9},{9,8},{10,11... | collective-permute-start | bytes 786440 | tf_op jit(solution)/shard_map/ppermute | solution.py:199
  31.7 5.4 %collective-permute-start.8 = (f32[512,128]{1,0:T(8,128)S(1)}, f32[512,128]{1,0:T(8,128)S(1)}, u32[]{:S(2)}, u32[]{:S(2)}) collective-permute-start(f32[512,128]{1,0:T(8,128)S(1)} %get-tuple-element.48), channel_id=1, source_target_pairs={{0,2},{1,3},{2,0},{3,1},{4,6},{5,7},{6,4},{7,5},{8,10},{9,11},{10,... | collective-permute-start | bytes 786440 | tf_op jit(solution)/shard_map/ppermute | solution.py:204
  37.1 6.2 %collective-permute-start.9 = (f32[512,128]{1,0:T(8,128)S(1)}, f32[512,128]{1,0:T(8,128)S(1)}, u32[]{:S(2)}, u32[]{:S(2)}) collective-permute-start(f32[512,128]{1,0:T(8,128)S(1)} %get-tuple-element.48), channel_id=1, source_target_pairs={{0,4},{1,5},{2,6},{3,7},{4,0},{5,1},{6,2},{7,3},{8,12},{9,13},{10,... | collective-permute-start | bytes 786440 | tf_op jit(solution)/shard_map/ppermute | solution.py:204
  45.4 2.7 %collective-permute-start.13 = (f32[512,128]{1,0:T(8,128)S(1)}, f32[512,128]{1,0:T(8,128)S(1)}, u32[]{:S(2)}, u32[]{:S(2)}) collective-permute-start(f32[512,128]{1,0:T(8,128)S(1)} %get-tuple-element.48), channel_id=1, source_target_pairs={{0,12},{1,13},{2,14},{3,15},{4,8},{5,9},{6,10},{7,11},{8,4},{9,5},... | collective-permute-start | bytes 786440 | tf_op jit(solution)/shard_map/ppermute | solution.py:204
  48.9 6.4 %collective-permute-done.9 = f32[512,128]{1,0:T(8,128)S(1)} collective-permute-done((f32[512,128]{1,0:T(8,128)S(1)}, f32[512,128]{1,0:T(8,128)S(1)}, u32[]{:S(2)}, u32[]{:S(2)}) %collective-permute-start.9) | collective-permute-done | bytes 262176 | tf_op jit(solution)/shard_map/ppermute | solution.py:204
  58.1 9.7 %collective-permute-done.11 = f32[512,128]{1,0:T(8,128)S(1)} collective-permute-done((f32[512,128]{1,0:T(8,128)S(1)}, f32[512,128]{1,0:T(8,128)S(1)}, u32[]{:S(2)}, u32[]{:S(2)}) %collective-permute-start.11) | collective-permute-done | bytes 262176 | tf_op jit(solution)/shard_map/ppermute | solution.py:204
  73.6 2.5 fusion.5
  77.8 2.5 fusion.8
  80.5 3.6 %collective-permute-start.16 = (f32[64,1152]{1,0:T(8,128)S(1)}, f32[64,1152]{1,0:T(8,128)S(1)}, u32[]{:S(2)}, u32[]{:S(2)}) collective-permute-start(f32[64,1152]{1,0:T(8,128)S(1)} %fusion.4), channel_id=1, source_target_pairs={{0,64},{16,80},{32,96},{48,112},{64,0},{80,16},{96,32},{112,48},{1... | collective-permute-start | bytes 884744 | tf_op jit(solution)/shard_map/ppermute | solution.py:209
  84.0 7.1 %fusion.2 = f32[1536,1024]{1,0:T(8,128)S(1)} fusion(f32[512,1024]{1,0:T(8,128)} %constant_dynamic-update-slice_fusion, f32[1024,1536]{1,0:T(8,128)S(1)} %bitcast.11, s32[]{:T(128)S(6)} %select_n.125), kind=kOutput, calls=%fused_computation.2 | convolution fusion | flops 4831838208 | bytes 11534340 | tf_op jit(solution)/shard_map/dot_general | solution.py:213
  92.8 7.1 %fusion = f32[1536,1024]{1,0:T(8,128)S(1)} fusion(f32[512,1024]{1,0:T(8,128)} %collective-permute-done.15, f32[1024,1536]{1,0:T(8,128)S(1)} %bitcast.11, s32[]{:T(128)S(6)} %select_n.126), kind=kOutput, calls=%fused_computation | convolution fusion | flops 4831838208 | bytes 11534340 | tf_op jit(solution)/shard_map/dot_general | solution.py:213
  99.9 2.2 add.172
  103.7 2.7 %collective-permute-start.25 = (f32[64,1152]{1,0:T(8,128)S(1)}, f32[64,1152]{1,0:T(8,128)S(1)}, u32[]{:S(2)}, u32[]{:S(2)}) collective-permute-start(f32[64,1152]{1,0:T(8,128)S(1)} %add.171), channel_id=1, source_target_pairs={{0,32},{16,48},{32,0},{48,16},{64,96},{80,112},{96,64},{112,80},{1... | collective-permute-start | bytes 884744 | tf_op jit(solution)/shard_map/ppermute | solution.py:209
  106.4 2.1 collective-permute-start.24
  108.4 2.0 collective-permute-start.23
  110.4 2.3 collective-permute-done.25
  112.7 2.5 collective-permute-start.28
  115.2 1.8 collective-permute-start.22
  117.0 5.7 %collective-permute-done.28 = f32[64,1152]{1,0:T(8,128)S(1)} collective-permute-done((f32[64,1152]{1,0:T(8,128)S(1)}, f32[64,1152]{1,0:T(8,128)S(1)}, u32[]{:S(2)}, u32[]{:S(2)}) %collective-permute-start.28) | collective-permute-done | bytes 294944 | tf_op jit(solution)/shard_map/ppermute | solution.py:204
  124.4 4.1 %collective-permute-start.21 = (f32[192,1024]{1,0:T(8,128)S(1)}, f32[192,1024]{1,0:T(8,128)S(1)}, u32[]{:S(2)}, u32[]{:S(2)}) collective-permute-start(f32[192,1024]{1,0:T(8,128)S(1)} %get-tuple-element.40), channel_id=1, source_target_pairs={{0,64},{16,80},{32,96},{48,112},{64,0},{80,16},{96,32},{112,48},{1... | collective-permute-start | bytes 2359304 | tf_op jit(solution)/shard_map/ppermute | solution.py:209
  128.5 2.1 collective-permute-done.26
  130.6 31.8 %collective-permute-done.24 = f32[192,1024]{1,0:T(8,128)S(1)} collective-permute-done((f32[192,1024]{1,0:T(8,128)S(1)}, f32[192,1024]{1,0:T(8,128)S(1)}, u32[]{:S(2)}, u32[]{:S(2)}) %collective-permute-start.24) | collective-permute-done | bytes 786464 | tf_op jit(solution)/shard_map/ppermute | solution.py:209
  162.3 3.9 %collective-permute-start.19 = (f32[192,1024]{1,0:T(8,128)S(1)}, f32[192,1024]{1,0:T(8,128)S(1)}, u32[]{:S(2)}, u32[]{:S(2)}) collective-permute-start(f32[192,1024]{1,0:T(8,128)S(1)} %get-tuple-element.38), channel_id=1, source_target_pairs={{0,32},{16,48},{32,0},{48,16},{64,96},{80,112},{96,64},{112,80},{1... | collective-permute-start | bytes 2359304 | tf_op jit(solution)/shard_map/ppermute | solution.py:209
  166.6 3.0 %collective-permute-start.29 = (f32[4,64,1152]{2,1,0:T(8,128)S(1)}, f32[4,64,1152]{2,1,0:T(8,128)S(1)}, u32[]{:S(2)}, u32[]{:S(2)}) collective-permute-start(f32[4,64,1152]{2,1,0:T(8,128)S(1)} %pad_maximum_fusion.mine_ref), channel_id=1, source_target_pairs={{0,1},{1,0},{2,3},{3,2},{4,5},{5,4},{6,7},{7,6},{8,9},{9,8},{10,11... | collective-permute-start | bytes 3538952 | tf_op jit(solution)/shard_map/ppermute | solution.py:199
  169.7 14.0 %collective-permute-done.21 = f32[192,1024]{1,0:T(8,128)S(1)} collective-permute-done((f32[192,1024]{1,0:T(8,128)S(1)}, f32[192,1024]{1,0:T(8,128)S(1)}, u32[]{:S(2)}, u32[]{:S(2)}) %collective-permute-start.21) | collective-permute-done | bytes 786464 | tf_op jit(solution)/shard_map/ppermute | solution.py:209
  183.7 8.6 %collective-permute-done.20 = f32[192,1024]{1,0:T(8,128)S(1)} collective-permute-done((f32[192,1024]{1,0:T(8,128)S(1)}, f32[192,1024]{1,0:T(8,128)S(1)}, u32[]{:S(2)}, u32[]{:S(2)}) %collective-permute-start.20) | collective-permute-done | bytes 786464 | tf_op jit(solution)/shard_map/ppermute | solution.py:209
  192.3 8.2 %collective-permute-done.18 = f32[192,1024]{1,0:T(8,128)S(1)} collective-permute-done((f32[192,1024]{1,0:T(8,128)S(1)}, f32[192,1024]{1,0:T(8,128)S(1)}, u32[]{:S(2)}, u32[]{:S(2)}) %collective-permute-start.18) | collective-permute-done | bytes 786464 | tf_op jit(solution)/shard_map/ppermute | solution.py:209
  201.2 48.3 %shard_map.28 = (f32[1024,1024]{1,0:T(8,128)S(1)}, f32[1024,128]{1,0:T(8,128)S(1)}) custom-call(s32[2]{0:T(128)S(1)} %pad_add_fusion.where_ref, f32[4,64,1152]{2,1,0:T(8,128)S(1)} %pad_maximum_fusion.mine_ref, f32[4,64,1152]{2,1,0:T(8,128)S(1)} %collective-permute-done.29.other_ref), custom_call_target="tpu_custom_call" | custom-call | flops 80000000000 | bytes 8388608 | tf_op jit(solution)/shard_map/pallas_call | solution.py:137
  249.5 4.6 %shard_map.29 = f32[192,1024]{1,0:T(8,128)} custom-call(f32[192,1024]{1,0:T(8,128)S(1)} %add_add_fusion.gram_ref, f32[1024,1024]{1,0:T(8,128)S(1)} %get-tuple-element.45.low_ref, f32[1024,128]{1,0:T(8,128)S(1)} %get-tuple-element.46.inv_ref), custom_call_target="tpu_custom_call" | custom-call | tf_op jit(solution)/shard_map/pallas_call | solution.py:174
  (69 shorter events, 31.7 us)
Async XLA Ops:
  0.0 11.9 %copy-start = (f32[1024]{0:T(1024)S(1)}, f32[1024]{0:T(1024)}, u32[]{:S(2)}) copy-start(f32[1024]{0:T(1024)} %param.3) | copy-start | bytes 12292
  3.1 7.4 %collective-permute-start.6 = (f32[1024,128]{1,0:T(8,128)}, f32[1024,128]{1,0:T(8,128)}, u32[]{:S(2)}, u32[]{:S(2)}) collective-permute-start(f32[1024,128]{1,0:T(8,128)} %get-tuple-element.63), channel_id=1, source_target_pairs={{0,14},{16,30},{32,46},{48,62},{64,78},{80,94},{96,110},{112,126}} | collective-permute-start | bytes 1572872 | tf_op jit(solution)/shard_map/ppermute | solution.py:227
  4.6 6.7 %collective-permute-start.5 = (f32[1024,128]{1,0:T(8,128)S(1)}, f32[1024,128]{1,0:T(8,128)}, u32[]{:S(2)}, u32[]{:S(2)}) collective-permute-start(f32[1024,128]{1,0:T(8,128)S(1)} %get-tuple-element.58), channel_id=1, source_target_pairs={{0,12},{16,28},{32,44},{48,60},{64,76},{80,92},{96,108},{112,124}} | collective-permute-start | bytes 1572872 | tf_op jit(solution)/shard_map/ppermute | solution.py:227
  6.0 11.9 %collective-permute-start.4 = (f32[1024,128]{1,0:T(8,128)S(1)}, f32[1024,128]{1,0:T(8,128)}, u32[]{:S(2)}, u32[]{:S(2)}) collective-permute-start(f32[1024,128]{1,0:T(8,128)S(1)} %get-tuple-element.59), channel_id=1, source_target_pairs={{0,10},{16,26},{32,42},{48,58},{64,74},{80,90},{96,106},{112,122}} | collective-permute-start | bytes 1572872 | tf_op jit(solution)/shard_map/ppermute | solution.py:227
  7.5 10.3 %collective-permute-start.3 = (f32[1024,128]{1,0:T(8,128)S(1)}, f32[1024,128]{1,0:T(8,128)}, u32[]{:S(2)}, u32[]{:S(2)}) collective-permute-start(f32[1024,128]{1,0:T(8,128)S(1)} %get-tuple-element.60), channel_id=1, source_target_pairs={{0,8},{16,24},{32,40},{48,56},{64,72},{80,88},{96,104},{112,120}} | collective-permute-start | bytes 1572872 | tf_op jit(solution)/shard_map/ppermute | solution.py:227
  9.0 8.8 %collective-permute-start.2 = (f32[1024,128]{1,0:T(8,128)S(1)}, f32[1024,128]{1,0:T(8,128)}, u32[]{:S(2)}, u32[]{:S(2)}) collective-permute-start(f32[1024,128]{1,0:T(8,128)S(1)} %get-tuple-element.61), channel_id=1, source_target_pairs={{0,6},{16,22},{32,38},{48,54},{64,70},{80,86},{96,102},{112,118}} | collective-permute-start | bytes 1572872 | tf_op jit(solution)/shard_map/ppermute | solution.py:227
  10.5 7.3 %collective-permute-start.1 = (f32[1024,128]{1,0:T(8,128)S(1)}, f32[1024,128]{1,0:T(8,128)S(1)}, u32[]{:S(2)}, u32[]{:S(2)}) collective-permute-start(f32[1024,128]{1,0:T(8,128)S(1)} %get-tuple-element.62), channel_id=1, source_target_pairs={{0,4},{16,20},{32,36},{48,52},{64,68},{80,84},{96,100},{112,116}} | collective-permute-start | bytes 1572872 | tf_op jit(solution)/shard_map/ppermute | solution.py:227
  11.2 6.6 %collective-permute-start = (f32[1024,128]{1,0:T(8,128)S(1)}, f32[1024,128]{1,0:T(8,128)S(1)}, u32[]{:S(2)}, u32[]{:S(2)}) collective-permute-start(f32[1024,128]{1,0:T(8,128)S(1)} %get-tuple-element.57), channel_id=1, source_target_pairs={{0,2},{16,18},{32,34},{48,50},{64,66},{80,82},{96,98},{112,114}} | collective-permute-start | bytes 1572872 | tf_op jit(solution)/shard_map/ppermute | solution.py:227
  20.1 9.3 %collective-permute-start.7 = (f32[512,128]{1,0:T(8,128)S(1)}, f32[512,128]{1,0:T(8,128)S(1)}, u32[]{:S(2)}, u32[]{:S(2)}) collective-permute-start(f32[512,128]{1,0:T(8,128)S(1)} %slice.45), channel_id=1, source_target_pairs={{0,1},{1,0},{2,3},{3,2},{4,5},{5,4},{6,7},{7,6},{8,9},{9,8},{10,11... | collective-permute-start | bytes 786440 | tf_op jit(solution)/shard_map/ppermute | solution.py:199
  31.7 13.6 %collective-permute-start.8 = (f32[512,128]{1,0:T(8,128)S(1)}, f32[512,128]{1,0:T(8,128)S(1)}, u32[]{:S(2)}, u32[]{:S(2)}) collective-permute-start(f32[512,128]{1,0:T(8,128)S(1)} %get-tuple-element.48), channel_id=1, source_target_pairs={{0,2},{1,3},{2,0},{3,1},{4,6},{5,7},{6,4},{7,5},{8,10},{9,11},{10,... | collective-permute-start | bytes 786440 | tf_op jit(solution)/shard_map/ppermute | solution.py:204
  37.1 18.2 %collective-permute-start.9 = (f32[512,128]{1,0:T(8,128)S(1)}, f32[512,128]{1,0:T(8,128)S(1)}, u32[]{:S(2)}, u32[]{:S(2)}) collective-permute-start(f32[512,128]{1,0:T(8,128)S(1)} %get-tuple-element.48), channel_id=1, source_target_pairs={{0,4},{1,5},{2,6},{3,7},{4,0},{5,1},{6,2},{7,3},{8,12},{9,13},{10,... | collective-permute-start | bytes 786440 | tf_op jit(solution)/shard_map/ppermute | solution.py:204
  43.3 14.0 %collective-permute-start.10 = (f32[512,128]{1,0:T(8,128)S(1)}, f32[512,128]{1,0:T(8,128)S(1)}, u32[]{:S(2)}, u32[]{:S(2)}) collective-permute-start(f32[512,128]{1,0:T(8,128)S(1)} %get-tuple-element.48), channel_id=1, source_target_pairs={{0,6},{1,7},{2,4},{3,5},{4,2},{5,3},{6,0},{7,1},{8,14},{9,15},{10,... | collective-permute-start | bytes 786440 | tf_op jit(solution)/shard_map/ppermute | solution.py:204
  43.6 24.2 %collective-permute-start.11 = (f32[512,128]{1,0:T(8,128)S(1)}, f32[512,128]{1,0:T(8,128)S(1)}, u32[]{:S(2)}, u32[]{:S(2)}) collective-permute-start(f32[512,128]{1,0:T(8,128)S(1)} %get-tuple-element.48), channel_id=1, source_target_pairs={{0,8},{1,9},{2,10},{3,11},{4,12},{5,13},{6,14},{7,15},{8,0},{9,1},... | collective-permute-start | bytes 786440 | tf_op jit(solution)/shard_map/ppermute | solution.py:204
  43.6 25.0 %collective-permute-start.12 = (f32[512,128]{1,0:T(8,128)S(1)}, f32[512,128]{1,0:T(8,128)S(1)}, u32[]{:S(2)}, u32[]{:S(2)}) collective-permute-start(f32[512,128]{1,0:T(8,128)S(1)} %get-tuple-element.48), channel_id=1, source_target_pairs={{0,10},{1,11},{2,8},{3,9},{4,14},{5,15},{6,12},{7,13},{8,2},{9,3},... | collective-permute-start | bytes 786440 | tf_op jit(solution)/shard_map/ppermute | solution.py:204
  45.4 24.0 %collective-permute-start.13 = (f32[512,128]{1,0:T(8,128)S(1)}, f32[512,128]{1,0:T(8,128)S(1)}, u32[]{:S(2)}, u32[]{:S(2)}) collective-permute-start(f32[512,128]{1,0:T(8,128)S(1)} %get-tuple-element.48), channel_id=1, source_target_pairs={{0,12},{1,13},{2,14},{3,15},{4,8},{5,9},{6,10},{7,11},{8,4},{9,5},... | collective-permute-start | bytes 786440 | tf_op jit(solution)/shard_map/ppermute | solution.py:204
  55.3 14.8 %collective-permute-start.14 = (f32[512,128]{1,0:T(8,128)S(1)}, f32[512,128]{1,0:T(8,128)S(1)}, u32[]{:S(2)}, u32[]{:S(2)}) collective-permute-start(f32[512,128]{1,0:T(8,128)S(1)} %get-tuple-element.48), channel_id=1, source_target_pairs={{0,14},{1,15},{2,12},{3,13},{4,10},{5,11},{6,8},{7,9},{8,6},{9,7},... | collective-permute-start | bytes 786440 | tf_op jit(solution)/shard_map/ppermute | solution.py:204
  68.6 15.4 %slice-start = ((s8[6291456]{0:T(1024)(128)(4,1)}), s8[2097152]{0:T(1024)(128)(4,1)S(1)}, s32[]{:S(2)}) async-start(s8[6291456]{0:T(1024)(128)(4,1)} %bitcast.10), calls=%async_computation | async-start | bytes 4194304
  70.9 5.5 %collective-permute-start.15 = (f32[512,1024]{1,0:T(8,128)}, f32[512,1024]{1,0:T(8,128)}, u32[]{:S(2)}, u32[]{:S(2)}) collective-permute-start(f32[512,1024]{1,0:T(8,128)} %constant_dynamic-update-slice_fusion), channel_id=1, source_target_pairs={{0,1},{1,0},{2,3},{3,2},{4,5},{5,4},{6,7},{7,6},{8,9},{9,8},{10,11... | collective-permute-start | bytes 6291464 | tf_op jit(solution)/shard_map/ppermute | solution.py:199
  80.5 10.7 %collective-permute-start.16 = (f32[64,1152]{1,0:T(8,128)S(1)}, f32[64,1152]{1,0:T(8,128)S(1)}, u32[]{:S(2)}, u32[]{:S(2)}) collective-permute-start(f32[64,1152]{1,0:T(8,128)S(1)} %fusion.4), channel_id=1, source_target_pairs={{0,64},{16,80},{32,96},{48,112},{64,0},{80,16},{96,32},{112,48},{1... | collective-permute-start | bytes 884744 | tf_op jit(solution)/shard_map/ppermute | solution.py:209
  91.2 11.5 %collective-permute-start.17 = (f32[64,1152]{1,0:T(8,128)S(1)}, f32[64,1152]{1,0:T(8,128)}, u32[]{:S(2)}, u32[]{:S(2)}) collective-permute-start(f32[64,1152]{1,0:T(8,128)S(1)} %add.170), channel_id=1, source_target_pairs={{0,16},{16,0},{32,48},{48,32},{64,80},{80,64},{96,112},{112,96},{1... | collective-permute-start | bytes 884744 | tf_op jit(solution)/shard_map/ppermute | solution.py:209
  103.7 9.0 %collective-permute-start.25 = (f32[64,1152]{1,0:T(8,128)S(1)}, f32[64,1152]{1,0:T(8,128)S(1)}, u32[]{:S(2)}, u32[]{:S(2)}) collective-permute-start(f32[64,1152]{1,0:T(8,128)S(1)} %add.171), channel_id=1, source_target_pairs={{0,32},{16,48},{32,0},{48,16},{64,96},{80,112},{96,64},{112,80},{1... | collective-permute-start | bytes 884744 | tf_op jit(solution)/shard_map/ppermute | solution.py:209
  106.4 56.0 %collective-permute-start.24 = (f32[192,1024]{1,0:T(8,128)S(1)}, f32[192,1024]{1,0:T(8,128)S(1)}, u32[]{:S(2)}, u32[]{:S(2)}) collective-permute-start(f32[192,1024]{1,0:T(8,128)S(1)} %get-tuple-element.43), channel_id=1, source_target_pairs={{0,112},{16,96},{32,80},{48,64},{64,48},{80,32},{96,16},{112,0},{1... | collective-permute-start | bytes 2359304 | tf_op jit(solution)/shard_map/ppermute | solution.py:209
  108.4 57.8 %collective-permute-start.23 = (f32[192,1024]{1,0:T(8,128)S(1)}, f32[192,1024]{1,0:T(8,128)S(1)}, u32[]{:S(2)}, u32[]{:S(2)}) collective-permute-start(f32[192,1024]{1,0:T(8,128)S(1)} %get-tuple-element.42), channel_id=1, source_target_pairs={{0,96},{16,112},{32,64},{48,80},{64,32},{80,48},{96,0},{112,16},{1... | collective-permute-start | bytes 2359304 | tf_op jit(solution)/shard_map/ppermute | solution.py:209
  112.7 10.0 %collective-permute-start.28 = (f32[64,1152]{1,0:T(8,128)S(1)}, f32[64,1152]{1,0:T(8,128)S(1)}, u32[]{:S(2)}, u32[]{:S(2)}) collective-permute-start(f32[64,1152]{1,0:T(8,128)S(1)} %add.188), channel_id=1, source_target_pairs={{0,6},{1,7},{2,4},{3,5},{4,2},{5,3},{6,0},{7,1},{8,14},{9,15},{10,... | collective-permute-start | bytes 884744 | tf_op jit(solution)/shard_map/ppermute | solution.py:204
  115.2 51.4 %collective-permute-start.22 = (f32[192,1024]{1,0:T(8,128)S(1)}, f32[192,1024]{1,0:T(8,128)S(1)}, u32[]{:S(2)}, u32[]{:S(2)}) collective-permute-start(f32[192,1024]{1,0:T(8,128)S(1)} %get-tuple-element.41), channel_id=1, source_target_pairs={{0,80},{16,64},{32,112},{48,96},{64,16},{80,0},{96,48},{112,32},{1... | collective-permute-start | bytes 2359304 | tf_op jit(solution)/shard_map/ppermute | solution.py:209
  117.0 7.4 %collective-permute-start.27 = (f32[64,1152]{1,0:T(8,128)S(1)}, f32[64,1152]{1,0:T(8,128)S(1)}, u32[]{:S(2)}, u32[]{:S(2)}) collective-permute-start(f32[64,1152]{1,0:T(8,128)S(1)} %add.188), channel_id=1, source_target_pairs={{0,4},{1,5},{2,6},{3,7},{4,0},{5,1},{6,2},{7,3},{8,12},{9,13},{10,... | collective-permute-start | bytes 884744 | tf_op jit(solution)/shard_map/ppermute | solution.py:204
  122.7 7.8 %collective-permute-start.26 = (f32[64,1152]{1,0:T(8,128)S(1)}, f32[64,1152]{1,0:T(8,128)S(1)}, u32[]{:S(2)}, u32[]{:S(2)}) collective-permute-start(f32[64,1152]{1,0:T(8,128)S(1)} %add.188), channel_id=1, source_target_pairs={{0,2},{1,3},{2,0},{3,1},{4,6},{5,7},{6,4},{7,5},{8,10},{9,11},{10,... | collective-permute-start | bytes 884744 | tf_op jit(solution)/shard_map/ppermute | solution.py:204
  124.4 59.3 %collective-permute-start.21 = (f32[192,1024]{1,0:T(8,128)S(1)}, f32[192,1024]{1,0:T(8,128)S(1)}, u32[]{:S(2)}, u32[]{:S(2)}) collective-permute-start(f32[192,1024]{1,0:T(8,128)S(1)} %get-tuple-element.40), channel_id=1, source_target_pairs={{0,64},{16,80},{32,96},{48,112},{64,0},{80,16},{96,32},{112,48},{1... | collective-permute-start | bytes 2359304 | tf_op jit(solution)/shard_map/ppermute | solution.py:209
  130.6 61.8 %collective-permute-start.20 = (f32[192,1024]{1,0:T(8,128)S(1)}, f32[192,1024]{1,0:T(8,128)S(1)}, u32[]{:S(2)}, u32[]{:S(2)}) collective-permute-start(f32[192,1024]{1,0:T(8,128)S(1)} %get-tuple-element.39), channel_id=1, source_target_pairs={{0,48},{16,32},{32,16},{48,0},{64,112},{80,96},{96,80},{112,64},{1... | collective-permute-start | bytes 2359304 | tf_op jit(solution)/shard_map/ppermute | solution.py:209
  162.3 30.0 %collective-permute-start.19 = (f32[192,1024]{1,0:T(8,128)S(1)}, f32[192,1024]{1,0:T(8,128)S(1)}, u32[]{:S(2)}, u32[]{:S(2)}) collective-permute-start(f32[192,1024]{1,0:T(8,128)S(1)} %get-tuple-element.38), channel_id=1, source_target_pairs={{0,32},{16,48},{32,0},{48,16},{64,96},{80,112},{96,64},{112,80},{1... | collective-permute-start | bytes 2359304 | tf_op jit(solution)/shard_map/ppermute | solution.py:209
  166.3 34.2 %collective-permute-start.18 = (f32[192,1024]{1,0:T(8,128)S(1)}, f32[192,1024]{1,0:T(8,128)S(1)}, u32[]{:S(2)}, u32[]{:S(2)}) collective-permute-start(f32[192,1024]{1,0:T(8,128)S(1)} %get-tuple-element.37), channel_id=1, source_target_pairs={{0,16},{16,0},{32,48},{48,32},{64,80},{80,64},{96,112},{112,96},{1... | collective-permute-start | bytes 2359304 | tf_op jit(solution)/shard_map/ppermute | solution.py:209
  166.6 34.6 %collective-permute-start.29 = (f32[4,64,1152]{2,1,0:T(8,128)S(1)}, f32[4,64,1152]{2,1,0:T(8,128)S(1)}, u32[]{:S(2)}, u32[]{:S(2)}) collective-permute-start(f32[4,64,1152]{2,1,0:T(8,128)S(1)} %pad_maximum_fusion.mine_ref), channel_id=1, source_target_pairs={{0,1},{1,0},{2,3},{3,2},{4,5},{5,4},{6,7},{7,6},{8,9},{9,8},{10,11... | collective-permute-start | bytes 3538952 | tf_op jit(solution)/shard_map/ppermute | solution.py:199
  (1 other events, 7.9 us)

commit v2 on v1

--- a/solution.py
+++ b/solution.py
@@ -225,16 +225,18 @@
     for j in range(1, CHIPS):
         pairs = [(o * UNK, o * UNK + 2 * j) for o in range(OBS)]
         chunk = chunk + lax.ppermute(design[:, j * BLOCK : (j + 1) * BLOCK], BOTH, pairs)
-    weighted = design * weights[:, None]
-    chunk, weighted = lax.optimization_barrier((chunk, weighted))
+
+    def core_half(half):
+        cut = lambda values: lax.dynamic_slice_in_dim(values, half * rows, rows, 0)
+        return cut(design) * cut(weights)[:, None]
+
+    chunk, first, second = lax.optimization_barrier((chunk, core_half(core), core_half(1 - core)))
     lower = swap_cores(chunk[rows:])
     part = jnp.where(core == 0, chunk[:rows], lower)
     mine = jnp.zeros((rows, WIDTH), jnp.float32)
     for k, got in enumerate(over_chips(part, CHIPS)):
         mine = lax.dynamic_update_slice(mine, got, (0, (chip ^ k) * BLOCK))
     other = swap_cores(mine)
-    first = lax.dynamic_slice_in_dim(weighted, core * rows, rows, 0)
-    second = lax.dynamic_slice_in_dim(weighted, (1 - core) * rows, rows, 0)
     first_weights = lax.dynamic_slice_in_dim(weights, core * rows, rows, 0)[:, None]
     second_weights = lax.dynamic_slice_in_dim(weights, (1 - core) * rows, rows, 0)[:, None]
 

time: 258 us -> 254 us (0.984)
  local copies, waits for them, and re-layouts: 13.4 us -> 5.69 us
  waiting for transfers between devices: 93.2 us -> 97.7 us
  matrix products: 19.2 us -> 16 us
  starting transfers between devices: 62.2 us -> 64.8 us
    dynamic_update_slice x7, local copies, waits for them, and re-layouts: 5.35 us -> 0.17 us  [local(): mine = lax.dynamic_update_slice(mine, got, (0, (chip ^ k) * BLOCK))]
    dot_general x4, matrix products: 19.2 us -> 16 us  [high_dot(): lax.dot_general(left, right, (((0,), (0,)), ((), ())), precision=lax.Prec...]
  transfers between devices with their start and end apart: 30 -> 30, of which waited for: 13 -> 15; matrix products, arithmetic and copies ran while one was open for 13% -> 9% of each run, Pallas kernels for 0% -> 0%
where the time goes in v2:
time: 254 us; the launch traced here: 250 us
  waiting for transfers between devices  97.7 us (38%)
  starting transfers between devices  64.8 us (26%)
  Pallas kernels  52.8 us (21%)
  matrix products  16 us (6%)
  other arithmetic  12.3 us (5%)
  local copies, waits for them, and re-layouts  5.69 us (2%)
    ppermute x10, waiting for transfers between devices, from_distance(): return lax.ppermute(value, 'obs', [(o, o ^ k) for o in range(OBS)])  66.4 us
    pallas_call x1, Pallas kernels, cholesky_parts(): pl.pallas_call(chol_kernel, out_shape=(jax.ShapeDtypeStruct((width, width...  48.3 us
    ppermute x10, waiting for transfers between devices, over_chips(): lax.ppermute(value, 'unk', [(u, u ^ 2 * k) for u in range(UNK)])  27.3 us
    ppermute x10, starting transfers between devices, from_distance(): return lax.ppermute(value, 'obs', [(o, o ^ k) for o in range(OBS)])  23.9 us
    ppermute x10, starting transfers between devices, over_chips(): lax.ppermute(value, 'unk', [(u, u ^ 2 * k) for u in range(UNK)])  20.5 us
    dot_general x4, matrix products, high_dot(): lax.dot_general(left, right, (((0,), (0,)), ((), ())), precision=lax.Prec...  16 us
    ppermute x3, starting transfers between devices, swap_cores(): return lax.ppermute(value, 'unk', [(u, u ^ 1) for u in range(UNK)])  11.6 us
    ppermute x7, starting transfers between devices, local(): lax.ppermute(design[:, j * BLOCK:(j + 1) * BLOCK], BOTH, pairs)  8.77 us
  transfers between devices with their start and end apart: 30, of which 15 were waited for; matrix products, arithmetic and copies ran while one was open for 9% of the time, Pallas kernels for 0%

profile of v2, /device:TPU:7, one launch (start us, length us, event | category | flops | bytes accessed | tf_op | source)
XLA Modules:
  0.0 249.6 jit_solution(17907931111761172869)
XLA Ops:
  0.0 3.1 %fusion.11 = (f32[1024,128]{1,0:T(8,128)S(1)}, f32[1024,128]{1,0:T(8,128)}, f32[1024,128]{1,0:T(8,128)S(1)}, f32[1024,128]{1,0:T(8,128)S(1)}, f32[1024,128]{1,0:...) fusion(f32[1024,1536]{1,0:T(8,128)} %param.2), kind=kLoop, calls=%fused_computation.42 | loop fusion | bytes 7340032 | tf_op jit(solution)/shard_map/slice | solution.py:227
  12.0 5.9 %dynamic-slice_multiply_fusion = (f32[512,1536]{1,0:T(8,128)}, f32[512,1536]{1,0:T(8,128)}) fusion(f32[1024,1536]{1,0:T(8,128)} %param.2, s32[]{:T(128)S(6)} %select_n.117, f32[512]{0:T(512)S(1)} %get-tuple-element.74, f32[512]{0:T(512)S(1)} %get-tuple-element.75, s32[]{:T(128)S(6)} %select_n.116), kind=kLoop, calls=%fused_computation | loop fusion | flops 1572864 | bytes 12587016 | tf_op jit(solution)/shard_map/mul | solution.py:231
  17.9 2.1 add_add_fusion.1
  20.1 8.1 %collective-permute-start.7 = (f32[512,128]{1,0:T(8,128)S(1)}, f32[512,128]{1,0:T(8,128)S(1)}, u32[]{:S(2)}, u32[]{:S(2)}) collective-permute-start(f32[512,128]{1,0:T(8,128)S(1)} %slice.45), channel_id=1, source_target_pairs={{0,1},{1,0},{2,3},{3,2},{4,5},{5,4},{6,7},{7,6},{8,9},{9,8},{10,11... | collective-permute-start | bytes 786440 | tf_op jit(solution)/shard_map/ppermute | solution.py:199
  29.6 5.4 %collective-permute-start.8 = (f32[512,128]{1,0:T(8,128)S(1)}, f32[512,128]{1,0:T(8,128)S(1)}, u32[]{:S(2)}, u32[]{:S(2)}) collective-permute-start(f32[512,128]{1,0:T(8,128)S(1)} %get-tuple-element.50), channel_id=1, source_target_pairs={{0,2},{1,3},{2,0},{3,1},{4,6},{5,7},{6,4},{7,5},{8,10},{9,11},{10,... | collective-permute-start | bytes 786440 | tf_op jit(solution)/shard_map/ppermute | solution.py:204
  35.1 6.3 %collective-permute-start.9 = (f32[512,128]{1,0:T(8,128)S(1)}, f32[512,128]{1,0:T(8,128)S(1)}, u32[]{:S(2)}, u32[]{:S(2)}) collective-permute-start(f32[512,128]{1,0:T(8,128)S(1)} %get-tuple-element.50), channel_id=1, source_target_pairs={{0,4},{1,5},{2,6},{3,7},{4,0},{5,1},{6,2},{7,3},{8,12},{9,13},{10,... | collective-permute-start | bytes 786440 | tf_op jit(solution)/shard_map/ppermute | solution.py:204
  43.4 2.8 %collective-permute-start.13 = (f32[512,128]{1,0:T(8,128)S(1)}, f32[512,128]{1,0:T(8,128)S(1)}, u32[]{:S(2)}, u32[]{:S(2)}) collective-permute-start(f32[512,128]{1,0:T(8,128)S(1)} %get-tuple-element.50), channel_id=1, source_target_pairs={{0,12},{1,13},{2,14},{3,15},{4,8},{5,9},{6,10},{7,11},{8,4},{9,5},... | collective-permute-start | bytes 786440 | tf_op jit(solution)/shard_map/ppermute | solution.py:204
  46.2 7.1 %collective-permute-done.9 = f32[512,128]{1,0:T(8,128)S(1)} collective-permute-done((f32[512,128]{1,0:T(8,128)S(1)}, f32[512,128]{1,0:T(8,128)S(1)}, u32[]{:S(2)}, u32[]{:S(2)}) %collective-permute-start.9) | collective-permute-done | bytes 262176 | tf_op jit(solution)/shard_map/ppermute | solution.py:204
  53.3 2.1 collective-permute-done.10
  55.5 10.3 %collective-permute-done.11 = f32[512,128]{1,0:T(8,128)S(1)} collective-permute-done((f32[512,128]{1,0:T(8,128)S(1)}, f32[512,128]{1,0:T(8,128)S(1)}, u32[]{:S(2)}, u32[]{:S(2)}) %collective-permute-start.11) | collective-permute-done | bytes 262176 | tf_op jit(solution)/shard_map/ppermute | solution.py:204
  69.2 2.8 %collective-permute-done.15 = f32[512,1024]{1,0:T(8,128)} collective-permute-done((f32[512,1024]{1,0:T(8,128)S(1)}, f32[512,1024]{1,0:T(8,128)}, u32[]{:S(2)}, u32[]{:S(2)}) %collective-permute-start.15) | collective-permute-done | bytes 2097184 | tf_op jit(solution)/shard_map/ppermute | solution.py:199
  73.2 2.5 %fusion.4 = f32[128,1024]{1,0:T(8,128)S(1)} fusion(f32[512,1024]{1,0:T(8,128)} %collective-permute-done.15, f32[512,64]{1,0:T(8,128)S(1)} %get-tuple-element.69, f32[512,64]{1,0:T(8,128)S(1)} %get-tuple-element.68, f32[512]{0:T(512)S(1)} %get-tuple-element.74), kind=kOutput, calls=%fused_computation.12 | convolution fusion | flops 402784256 | bytes 2885632 | tf_op jit(solution)/shard_map/dot_general | solution.py:213
  75.9 3.6 %collective-permute-start.16 = (f32[64,1152]{1,0:T(8,128)S(1)}, f32[64,1152]{1,0:T(8,128)S(1)}, u32[]{:S(2)}, u32[]{:S(2)}) collective-permute-start(f32[64,1152]{1,0:T(8,128)S(1)} %fusion), channel_id=1, source_target_pairs={{0,64},{16,80},{32,96},{48,112},{64,0},{80,16},{96,32},{112,48},{1... | collective-permute-start | bytes 884744 | tf_op jit(solution)/shard_map/ppermute | solution.py:209
  79.4 5.5 %fusion.14 = f32[1536,1024]{1,0:T(8,128)S(1)} fusion(f32[512,1536]{1,0:T(8,128)S(1)} %copy-done.1, f32[512,1024]{1,0:T(8,128)S(1)} %constant_dynamic-update-slice_fusion), kind=kOutput, calls=%fused_computation.45 | convolution fusion | flops 4831838208 | bytes 11534336 | tf_op jit(solution)/shard_map/dot_general | solution.py:213
  88.1 7.1 %fusion.15 = f32[1536,1024]{1,0:T(8,128)S(1)} fusion(f32[512,1536]{1,0:T(8,128)S(1)} %copy-done, f32[512,1024]{1,0:T(8,128)} %collective-permute-done.15), kind=kOutput, calls=%fused_computation.46 | convolution fusion | flops 4831838208 | bytes 11534336 | tf_op jit(solution)/shard_map/dot_general | solution.py:213
  95.2 2.2 add.174
  99.0 2.7 %collective-permute-start.25 = (f32[64,1152]{1,0:T(8,128)S(1)}, f32[64,1152]{1,0:T(8,128)S(1)}, u32[]{:S(2)}, u32[]{:S(2)}) collective-permute-start(f32[64,1152]{1,0:T(8,128)S(1)} %add.173), channel_id=1, source_target_pairs={{0,32},{16,48},{32,0},{48,16},{64,96},{80,112},{96,64},{112,80},{1... | collective-permute-start | bytes 884744 | tf_op jit(solution)/shard_map/ppermute | solution.py:209
  101.7 2.3 collective-permute-start.24
  105.7 2.2 collective-permute-done.25
  107.9 2.7 %collective-permute-start.28 = (f32[64,1152]{1,0:T(8,128)S(1)}, f32[64,1152]{1,0:T(8,128)S(1)}, u32[]{:S(2)}, u32[]{:S(2)}) collective-permute-start(f32[64,1152]{1,0:T(8,128)S(1)} %add.190), channel_id=1, source_target_pairs={{0,6},{1,7},{2,4},{3,5},{4,2},{5,3},{6,0},{7,1},{8,14},{9,15},{10,... | collective-permute-start | bytes 884744 | tf_op jit(solution)/shard_map/ppermute | solution.py:204
  110.7 2.3 collective-permute-start.22
  114.2 3.6 %collective-permute-done.28 = f32[64,1152]{1,0:T(8,128)S(1)} collective-permute-done((f32[64,1152]{1,0:T(8,128)S(1)}, f32[64,1152]{1,0:T(8,128)S(1)}, u32[]{:S(2)}, u32[]{:S(2)}) %collective-permute-start.28) | collective-permute-done | bytes 294944 | tf_op jit(solution)/shard_map/ppermute | solution.py:204
  117.7 2.7 %collective-permute-done.27 = f32[64,1152]{1,0:T(8,128)S(1)} collective-permute-done((f32[64,1152]{1,0:T(8,128)S(1)}, f32[64,1152]{1,0:T(8,128)S(1)}, u32[]{:S(2)}, u32[]{:S(2)}) %collective-permute-start.27) | collective-permute-done | bytes 294944 | tf_op jit(solution)/shard_map/ppermute | solution.py:204
  120.4 5.3 %collective-permute-start.21 = (f32[192,1024]{1,0:T(8,128)S(1)}, f32[192,1024]{1,0:T(8,128)S(1)}, u32[]{:S(2)}, u32[]{:S(2)}) collective-permute-start(f32[192,1024]{1,0:T(8,128)S(1)} %get-tuple-element.42), channel_id=1, source_target_pairs={{0,64},{16,80},{32,96},{48,112},{64,0},{80,16},{96,32},{112,48},{1... | collective-permute-start | bytes 2359304 | tf_op jit(solution)/shard_map/ppermute | solution.py:209
  126.2 31.6 %collective-permute-done.24 = f32[192,1024]{1,0:T(8,128)S(1)} collective-permute-done((f32[192,1024]{1,0:T(8,128)S(1)}, f32[192,1024]{1,0:T(8,128)S(1)}, u32[]{:S(2)}, u32[]{:S(2)}) %collective-permute-start.24) | collective-permute-done | bytes 786464 | tf_op jit(solution)/shard_map/ppermute | solution.py:209
  157.8 3.0 %collective-permute-start.19 = (f32[192,1024]{1,0:T(8,128)S(1)}, f32[192,1024]{1,0:T(8,128)S(1)}, u32[]{:S(2)}, u32[]{:S(2)}) collective-permute-start(f32[192,1024]{1,0:T(8,128)S(1)} %get-tuple-element.40), channel_id=1, source_target_pairs={{0,32},{16,48},{32,0},{48,16},{64,96},{80,112},{96,64},{112,80},{1... | collective-permute-start | bytes 2359304 | tf_op jit(solution)/shard_map/ppermute | solution.py:209
  162.1 2.6 %collective-permute-start.29 = (f32[4,64,1152]{2,1,0:T(8,128)S(1)}, f32[4,64,1152]{2,1,0:T(8,128)S(1)}, u32[]{:S(2)}, u32[]{:S(2)}) collective-permute-start(f32[4,64,1152]{2,1,0:T(8,128)S(1)} %pad_maximum_fusion.mine_ref), channel_id=1, source_target_pairs={{0,1},{1,0},{2,3},{3,2},{4,5},{5,4},{6,7},{7,6},{8,9},{9,8},{10,11... | collective-permute-start | bytes 3538952 | tf_op jit(solution)/shard_map/ppermute | solution.py:199
  164.8 14.5 %collective-permute-done.21 = f32[192,1024]{1,0:T(8,128)S(1)} collective-permute-done((f32[192,1024]{1,0:T(8,128)S(1)}, f32[192,1024]{1,0:T(8,128)S(1)}, u32[]{:S(2)}, u32[]{:S(2)}) %collective-permute-start.21) | collective-permute-done | bytes 786464 | tf_op jit(solution)/shard_map/ppermute | solution.py:209
  179.3 8.4 %collective-permute-done.20 = f32[192,1024]{1,0:T(8,128)S(1)} collective-permute-done((f32[192,1024]{1,0:T(8,128)S(1)}, f32[192,1024]{1,0:T(8,128)S(1)}, u32[]{:S(2)}, u32[]{:S(2)}) %collective-permute-start.20) | collective-permute-done | bytes 786464 | tf_op jit(solution)/shard_map/ppermute | solution.py:209
  187.7 8.3 %collective-permute-done.18 = f32[192,1024]{1,0:T(8,128)S(1)} collective-permute-done((f32[192,1024]{1,0:T(8,128)S(1)}, f32[192,1024]{1,0:T(8,128)S(1)}, u32[]{:S(2)}, u32[]{:S(2)}) %collective-permute-start.18) | collective-permute-done | bytes 786464 | tf_op jit(solution)/shard_map/ppermute | solution.py:209
  196.7 48.3 %shard_map.28 = (f32[1024,1024]{1,0:T(8,128)S(1)}, f32[1024,128]{1,0:T(8,128)S(1)}) custom-call(s32[2]{0:T(128)S(1)} %pad_add_fusion.where_ref, f32[4,64,1152]{2,1,0:T(8,128)S(1)} %pad_maximum_fusion.mine_ref, f32[4,64,1152]{2,1,0:T(8,128)S(1)} %collective-permute-done.29.other_ref), custom_call_target="tpu_custom_call" | custom-call | flops 80000000000 | bytes 8388608 | tf_op jit(solution)/shard_map/pallas_call | solution.py:137
  245.0 4.6 %shard_map.29 = f32[192,1024]{1,0:T(8,128)} custom-call(f32[192,1024]{1,0:T(8,128)S(1)} %add_add_fusion.gram_ref, f32[1024,1024]{1,0:T(8,128)S(1)} %get-tuple-element.47.low_ref, f32[1024,128]{1,0:T(8,128)S(1)} %get-tuple-element.48.inv_ref), custom_call_target="tpu_custom_call" | custom-call | tf_op jit(solution)/shard_map/pallas_call | solution.py:174
  (68 shorter events, 27.3 us)
Async XLA Ops:
  0.0 10.5 %copy-start.2 = (f32[1024]{0:T(1024)S(1)}, f32[1024]{0:T(1024)}, u32[]{:S(2)}) copy-start(f32[1024]{0:T(1024)} %param.3) | copy-start | bytes 12292
  3.1 7.5 %collective-permute-start.6 = (f32[1024,128]{1,0:T(8,128)}, f32[1024,128]{1,0:T(8,128)}, u32[]{:S(2)}, u32[]{:S(2)}) collective-permute-start(f32[1024,128]{1,0:T(8,128)} %get-tuple-element.62), channel_id=1, source_target_pairs={{0,14},{16,30},{32,46},{48,62},{64,78},{80,94},{96,110},{112,126}} | collective-permute-start | bytes 1572872 | tf_op jit(solution)/shard_map/ppermute | solution.py:227
  4.6 6.7 %collective-permute-start.5 = (f32[1024,128]{1,0:T(8,128)S(1)}, f32[1024,128]{1,0:T(8,128)}, u32[]{:S(2)}, u32[]{:S(2)}) collective-permute-start(f32[1024,128]{1,0:T(8,128)S(1)} %get-tuple-element.63), channel_id=1, source_target_pairs={{0,12},{16,28},{32,44},{48,60},{64,76},{80,92},{96,108},{112,124}} | collective-permute-start | bytes 1572872 | tf_op jit(solution)/shard_map/ppermute | solution.py:227
  6.0 11.9 %collective-permute-start.4 = (f32[1024,128]{1,0:T(8,128)S(1)}, f32[1024,128]{1,0:T(8,128)}, u32[]{:S(2)}, u32[]{:S(2)}) collective-permute-start(f32[1024,128]{1,0:T(8,128)S(1)} %get-tuple-element.64), channel_id=1, source_target_pairs={{0,10},{16,26},{32,42},{48,58},{64,74},{80,90},{96,106},{112,122}} | collective-permute-start | bytes 1572872 | tf_op jit(solution)/shard_map/ppermute | solution.py:227
  7.5 10.4 %collective-permute-start.3 = (f32[1024,128]{1,0:T(8,128)S(1)}, f32[1024,128]{1,0:T(8,128)}, u32[]{:S(2)}, u32[]{:S(2)}) collective-permute-start(f32[1024,128]{1,0:T(8,128)S(1)} %get-tuple-element.65), channel_id=1, source_target_pairs={{0,8},{16,24},{32,40},{48,56},{64,72},{80,88},{96,104},{112,120}} | collective-permute-start | bytes 1572872 | tf_op jit(solution)/shard_map/ppermute | solution.py:227
  9.0 8.9 %collective-permute-start.2 = (f32[1024,128]{1,0:T(8,128)S(1)}, f32[1024,128]{1,0:T(8,128)}, u32[]{:S(2)}, u32[]{:S(2)}) collective-permute-start(f32[1024,128]{1,0:T(8,128)S(1)} %get-tuple-element.66), channel_id=1, source_target_pairs={{0,6},{16,22},{32,38},{48,54},{64,70},{80,86},{96,102},{112,118}} | collective-permute-start | bytes 1572872 | tf_op jit(solution)/shard_map/ppermute | solution.py:227
  10.6 7.3 %collective-permute-start.1 = (f32[1024,128]{1,0:T(8,128)S(1)}, f32[1024,128]{1,0:T(8,128)S(1)}, u32[]{:S(2)}, u32[]{:S(2)}) collective-permute-start(f32[1024,128]{1,0:T(8,128)S(1)} %get-tuple-element.67), channel_id=1, source_target_pairs={{0,4},{16,20},{32,36},{48,52},{64,68},{80,84},{96,100},{112,116}} | collective-permute-start | bytes 1572872 | tf_op jit(solution)/shard_map/ppermute | solution.py:227
  11.3 6.6 %collective-permute-start = (f32[1024,128]{1,0:T(8,128)S(1)}, f32[1024,128]{1,0:T(8,128)S(1)}, u32[]{:S(2)}, u32[]{:S(2)}) collective-permute-start(f32[1024,128]{1,0:T(8,128)S(1)} %get-tuple-element.61), channel_id=1, source_target_pairs={{0,2},{16,18},{32,34},{48,50},{64,66},{80,82},{96,98},{112,114}} | collective-permute-start | bytes 1572872 | tf_op jit(solution)/shard_map/ppermute | solution.py:227
  20.1 9.3 %collective-permute-start.7 = (f32[512,128]{1,0:T(8,128)S(1)}, f32[512,128]{1,0:T(8,128)S(1)}, u32[]{:S(2)}, u32[]{:S(2)}) collective-permute-start(f32[512,128]{1,0:T(8,128)S(1)} %slice.45), channel_id=1, source_target_pairs={{0,1},{1,0},{2,3},{3,2},{4,5},{5,4},{6,7},{7,6},{8,9},{9,8},{10,11... | collective-permute-start | bytes 786440 | tf_op jit(solution)/shard_map/ppermute | solution.py:199
  29.6 13.7 %collective-permute-start.8 = (f32[512,128]{1,0:T(8,128)S(1)}, f32[512,128]{1,0:T(8,128)S(1)}, u32[]{:S(2)}, u32[]{:S(2)}) collective-permute-start(f32[512,128]{1,0:T(8,128)S(1)} %get-tuple-element.50), channel_id=1, source_target_pairs={{0,2},{1,3},{2,0},{3,1},{4,6},{5,7},{6,4},{7,5},{8,10},{9,11},{10,... | collective-permute-start | bytes 786440 | tf_op jit(solution)/shard_map/ppermute | solution.py:204
  35.1 18.2 %collective-permute-start.9 = (f32[512,128]{1,0:T(8,128)S(1)}, f32[512,128]{1,0:T(8,128)S(1)}, u32[]{:S(2)}, u32[]{:S(2)}) collective-permute-start(f32[512,128]{1,0:T(8,128)S(1)} %get-tuple-element.50), channel_id=1, source_target_pairs={{0,4},{1,5},{2,6},{3,7},{4,0},{5,1},{6,2},{7,3},{8,12},{9,13},{10,... | collective-permute-start | bytes 786440 | tf_op jit(solution)/shard_map/ppermute | solution.py:204
  41.4 14.0 %collective-permute-start.10 = (f32[512,128]{1,0:T(8,128)S(1)}, f32[512,128]{1,0:T(8,128)S(1)}, u32[]{:S(2)}, u32[]{:S(2)}) collective-permute-start(f32[512,128]{1,0:T(8,128)S(1)} %get-tuple-element.50), channel_id=1, source_target_pairs={{0,6},{1,7},{2,4},{3,5},{4,2},{5,3},{6,0},{7,1},{8,14},{9,15},{10,... | collective-permute-start | bytes 786440 | tf_op jit(solution)/shard_map/ppermute | solution.py:204
  41.6 24.2 %collective-permute-start.11 = (f32[512,128]{1,0:T(8,128)S(1)}, f32[512,128]{1,0:T(8,128)S(1)}, u32[]{:S(2)}, u32[]{:S(2)}) collective-permute-start(f32[512,128]{1,0:T(8,128)S(1)} %get-tuple-element.50), channel_id=1, source_target_pairs={{0,8},{1,9},{2,10},{3,11},{4,12},{5,13},{6,14},{7,15},{8,0},{9,1},... | collective-permute-start | bytes 786440 | tf_op jit(solution)/shard_map/ppermute | solution.py:204
  41.6 24.2 %collective-permute-start.12 = (f32[512,128]{1,0:T(8,128)S(1)}, f32[512,128]{1,0:T(8,128)S(1)}, u32[]{:S(2)}, u32[]{:S(2)}) collective-permute-start(f32[512,128]{1,0:T(8,128)S(1)} %get-tuple-element.50), channel_id=1, source_target_pairs={{0,10},{1,11},{2,8},{3,9},{4,14},{5,15},{6,12},{7,13},{8,2},{9,3},... | collective-permute-start | bytes 786440 | tf_op jit(solution)/shard_map/ppermute | solution.py:204
  43.4 22.5 %collective-permute-start.13 = (f32[512,128]{1,0:T(8,128)S(1)}, f32[512,128]{1,0:T(8,128)S(1)}, u32[]{:S(2)}, u32[]{:S(2)}) collective-permute-start(f32[512,128]{1,0:T(8,128)S(1)} %get-tuple-element.50), channel_id=1, source_target_pairs={{0,12},{1,13},{2,14},{3,15},{4,8},{5,9},{6,10},{7,11},{8,4},{9,5},... | collective-permute-start | bytes 786440 | tf_op jit(solution)/shard_map/ppermute | solution.py:204
  53.3 13.8 %collective-permute-start.14 = (f32[512,128]{1,0:T(8,128)S(1)}, f32[512,128]{1,0:T(8,128)S(1)}, u32[]{:S(2)}, u32[]{:S(2)}) collective-permute-start(f32[512,128]{1,0:T(8,128)S(1)} %get-tuple-element.50), channel_id=1, source_target_pairs={{0,14},{1,15},{2,12},{3,13},{4,10},{5,11},{6,8},{7,9},{8,6},{9,7},... | collective-permute-start | bytes 786440 | tf_op jit(solution)/shard_map/ppermute | solution.py:204
  67.1 4.8 %collective-permute-start.15 = (f32[512,1024]{1,0:T(8,128)S(1)}, f32[512,1024]{1,0:T(8,128)}, u32[]{:S(2)}, u32[]{:S(2)}) collective-permute-start(f32[512,1024]{1,0:T(8,128)S(1)} %constant_dynamic-update-slice_fusion), channel_id=1, source_target_pairs={{0,1},{1,0},{2,3},{3,2},{4,5},{5,4},{6,7},{7,6},{8,9},{9,8},{10,11... | collective-permute-start | bytes 6291464 | tf_op jit(solution)/shard_map/ppermute | solution.py:199
  75.9 10.6 %collective-permute-start.16 = (f32[64,1152]{1,0:T(8,128)S(1)}, f32[64,1152]{1,0:T(8,128)S(1)}, u32[]{:S(2)}, u32[]{:S(2)}) collective-permute-start(f32[64,1152]{1,0:T(8,128)S(1)} %fusion), channel_id=1, source_target_pairs={{0,64},{16,80},{32,96},{48,112},{64,0},{80,16},{96,32},{112,48},{1... | collective-permute-start | bytes 884744 | tf_op jit(solution)/shard_map/ppermute | solution.py:209
  79.4 8.6 %copy-start = (f32[512,1536]{1,0:T(8,128)S(1)}, f32[512,1536]{1,0:T(8,128)}, u32[]{:S(2)}) copy-start(f32[512,1536]{1,0:T(8,128)} %get-tuple-element.36) | copy-start | bytes 9437188
  86.5 11.5 %collective-permute-start.17 = (f32[64,1152]{1,0:T(8,128)S(1)}, f32[64,1152]{1,0:T(8,128)}, u32[]{:S(2)}, u32[]{:S(2)}) collective-permute-start(f32[64,1152]{1,0:T(8,128)S(1)} %add.172), channel_id=1, source_target_pairs={{0,16},{16,0},{32,48},{48,32},{64,80},{80,64},{96,112},{112,96},{1... | collective-permute-start | bytes 884744 | tf_op jit(solution)/shard_map/ppermute | solution.py:209
  99.0 8.9 %collective-permute-start.25 = (f32[64,1152]{1,0:T(8,128)S(1)}, f32[64,1152]{1,0:T(8,128)S(1)}, u32[]{:S(2)}, u32[]{:S(2)}) collective-permute-start(f32[64,1152]{1,0:T(8,128)S(1)} %add.173), channel_id=1, source_target_pairs={{0,32},{16,48},{32,0},{48,16},{64,96},{80,112},{96,64},{112,80},{1... | collective-permute-start | bytes 884744 | tf_op jit(solution)/shard_map/ppermute | solution.py:209
  101.7 56.1 %collective-permute-start.24 = (f32[192,1024]{1,0:T(8,128)S(1)}, f32[192,1024]{1,0:T(8,128)S(1)}, u32[]{:S(2)}, u32[]{:S(2)}) collective-permute-start(f32[192,1024]{1,0:T(8,128)S(1)} %get-tuple-element.45), channel_id=1, source_target_pairs={{0,112},{16,96},{32,80},{48,64},{64,48},{80,32},{96,16},{112,0},{1... | collective-permute-start | bytes 2359304 | tf_op jit(solution)/shard_map/ppermute | solution.py:209
  104.0 56.8 %collective-permute-start.23 = (f32[192,1024]{1,0:T(8,128)S(1)}, f32[192,1024]{1,0:T(8,128)S(1)}, u32[]{:S(2)}, u32[]{:S(2)}) collective-permute-start(f32[192,1024]{1,0:T(8,128)S(1)} %get-tuple-element.44), channel_id=1, source_target_pairs={{0,96},{16,112},{32,64},{48,80},{64,32},{80,48},{96,0},{112,16},{1... | collective-permute-start | bytes 2359304 | tf_op jit(solution)/shard_map/ppermute | solution.py:209
  107.9 9.8 %collective-permute-start.28 = (f32[64,1152]{1,0:T(8,128)S(1)}, f32[64,1152]{1,0:T(8,128)S(1)}, u32[]{:S(2)}, u32[]{:S(2)}) collective-permute-start(f32[64,1152]{1,0:T(8,128)S(1)} %add.190), channel_id=1, source_target_pairs={{0,6},{1,7},{2,4},{3,5},{4,2},{5,3},{6,0},{7,1},{8,14},{9,15},{10,... | collective-permute-start | bytes 884744 | tf_op jit(solution)/shard_map/ppermute | solution.py:204
  110.7 51.4 %collective-permute-start.22 = (f32[192,1024]{1,0:T(8,128)S(1)}, f32[192,1024]{1,0:T(8,128)S(1)}, u32[]{:S(2)}, u32[]{:S(2)}) collective-permute-start(f32[192,1024]{1,0:T(8,128)S(1)} %get-tuple-element.43), channel_id=1, source_target_pairs={{0,80},{16,64},{32,112},{48,96},{64,16},{80,0},{96,48},{112,32},{1... | collective-permute-start | bytes 2359304 | tf_op jit(solution)/shard_map/ppermute | solution.py:209
  113.0 7.4 %collective-permute-start.27 = (f32[64,1152]{1,0:T(8,128)S(1)}, f32[64,1152]{1,0:T(8,128)S(1)}, u32[]{:S(2)}, u32[]{:S(2)}) collective-permute-start(f32[64,1152]{1,0:T(8,128)S(1)} %add.190), channel_id=1, source_target_pairs={{0,4},{1,5},{2,6},{3,7},{4,0},{5,1},{6,2},{7,3},{8,12},{9,13},{10,... | collective-permute-start | bytes 884744 | tf_op jit(solution)/shard_map/ppermute | solution.py:204
  117.7 8.3 %collective-permute-start.26 = (f32[64,1152]{1,0:T(8,128)S(1)}, f32[64,1152]{1,0:T(8,128)S(1)}, u32[]{:S(2)}, u32[]{:S(2)}) collective-permute-start(f32[64,1152]{1,0:T(8,128)S(1)} %add.190), channel_id=1, source_target_pairs={{0,2},{1,3},{2,0},{3,1},{4,6},{5,7},{6,4},{7,5},{8,10},{9,11},{10,... | collective-permute-start | bytes 884744 | tf_op jit(solution)/shard_map/ppermute | solution.py:204
  120.4 58.9 %collective-permute-start.21 = (f32[192,1024]{1,0:T(8,128)S(1)}, f32[192,1024]{1,0:T(8,128)S(1)}, u32[]{:S(2)}, u32[]{:S(2)}) collective-permute-start(f32[192,1024]{1,0:T(8,128)S(1)} %get-tuple-element.42), channel_id=1, source_target_pairs={{0,64},{16,80},{32,96},{48,112},{64,0},{80,16},{96,32},{112,48},{1... | collective-permute-start | bytes 2359304 | tf_op jit(solution)/shard_map/ppermute | solution.py:209
  126.1 61.6 %collective-permute-start.20 = (f32[192,1024]{1,0:T(8,128)S(1)}, f32[192,1024]{1,0:T(8,128)S(1)}, u32[]{:S(2)}, u32[]{:S(2)}) collective-permute-start(f32[192,1024]{1,0:T(8,128)S(1)} %get-tuple-element.41), channel_id=1, source_target_pairs={{0,48},{16,32},{32,16},{48,0},{64,112},{80,96},{96,80},{112,64},{1... | collective-permute-start | bytes 2359304 | tf_op jit(solution)/shard_map/ppermute | solution.py:209
  157.8 29.9 %collective-permute-start.19 = (f32[192,1024]{1,0:T(8,128)S(1)}, f32[192,1024]{1,0:T(8,128)S(1)}, u32[]{:S(2)}, u32[]{:S(2)}) collective-permute-start(f32[192,1024]{1,0:T(8,128)S(1)} %get-tuple-element.40), channel_id=1, source_target_pairs={{0,32},{16,48},{32,0},{48,16},{64,96},{80,112},{96,64},{112,80},{1... | collective-permute-start | bytes 2359304 | tf_op jit(solution)/shard_map/ppermute | solution.py:209
  160.8 35.2 %collective-permute-start.18 = (f32[192,1024]{1,0:T(8,128)S(1)}, f32[192,1024]{1,0:T(8,128)S(1)}, u32[]{:S(2)}, u32[]{:S(2)}) collective-permute-start(f32[192,1024]{1,0:T(8,128)S(1)} %get-tuple-element.39), channel_id=1, source_target_pairs={{0,16},{16,0},{32,48},{48,32},{64,80},{80,64},{96,112},{112,96},{1... | collective-permute-start | bytes 2359304 | tf_op jit(solution)/shard_map/ppermute | solution.py:209
  162.1 34.6 %collective-permute-start.29 = (f32[4,64,1152]{2,1,0:T(8,128)S(1)}, f32[4,64,1152]{2,1,0:T(8,128)S(1)}, u32[]{:S(2)}, u32[]{:S(2)}) collective-permute-start(f32[4,64,1152]{2,1,0:T(8,128)S(1)} %pad_maximum_fusion.mine_ref), channel_id=1, source_target_pairs={{0,1},{1,0},{2,3},{3,2},{4,5},{5,4},{6,7},{7,6},{8,9},{9,8},{10,11... | collective-permute-start | bytes 3538952 | tf_op jit(solution)/shard_map/ppermute | solution.py:199
  (1 other events, 3.8 us)
